TPU v7x, 128 devices: a whole 4x4x4 slice. The times are simulated.
128 devices in a mesh: wide: 8 (over z_lo, x), narrow: 16 (over y, z_hi, core).
Axes of the slice: x: 4, y: 4, z: 4 (z_hi: 2, z_lo: 2; z = z_hi * 2 + z_lo), core: 2. Of those that a mesh axis runs over, the one named last changes fastest.
Arguments:
- seafloor_ops: bfloat16 [512, 4, 2, 128, 2048], P(None, None, None, 'wide', 'narrow'), may hold values from -0.25 to 0.25
- sensor_data: bfloat16 [512, 4, 2, 256], P('wide', None, None, 'narrow'), may hold values from -6 to 6
- column_freq: int32 [256], replicated, may hold values from 0 to 3
- row_owner: int32 [512], replicated, may hold values from 0 to 511, each once
- coef_class: int32 [128, 2048], P('wide', 'narrow'), may hold values from 0 to 7
- coef_table: float32 [8], replicated, may hold values from 0.02 to 0.24
Outputs:
- hessian_cols: bfloat16 [512, 4, 2, 256], P('wide', None, None, 'narrow')
- prior_field: bfloat16 [256, 128, 2048], P(None, 'wide', 'narrow')
All inputs are finite; a program needn't handle non-finite values.
Results may differ from a plain program's by a relative error of at most 0.0026.
Values may be sent and summed in bfloat16 or wider, within the bound.
No kernel may reach another device: no remote copies, remote signals or barrier semaphores. Data moves between devices by JAX's collectives and lax.ppermute only.
A program may use at most 128 MiB of HBM per device.

v0:
```python
import jax
import jax.numpy as jnp
from jax import lax
from jax.sharding import PartitionSpec as P

SWEEPS = 3


def extended(value, sides, width):
    for axis, dim in sides:
        size, length = (lax.axis_size(axis), value.shape[dim])
        up = [(i, (i + 1) % size) for i in range(size - 1)]
        down = [(j, i) for i, j in up]
        last = lax.slice_in_dim(value, length - width, length, axis=dim)
        initial = lax.slice_in_dim(value, 0, width, axis=dim)
        before = lax.ppermute(last, axis, up)
        after = lax.ppermute(initial, axis, down)
        value = jnp.concatenate([before, value, after], axis=dim)
    return value


def sweep(padded, coef):
    center = padded[:, 1:-1, 1:-1]
    inner = coef[1:-1, 1:-1]
    change = jnp.minimum(inner, coef[2:, 1:-1]) * (padded[:, 2:, 1:-1] - center)
    change = change + jnp.minimum(inner, coef[:-2, 1:-1]) * (padded[:, :-2, 1:-1] - center)
    change = change + jnp.minimum(inner, coef[1:-1, 2:]) * (padded[:, 1:-1, 2:] - center)
    change = change + jnp.minimum(inner, coef[1:-1, :-2]) * (padded[:, 1:-1, :-2] - center)
    return center + change


def on_device(seafloor_ops, sensor_data, column_freq, row_owner, coef_class, coef_table):
    sens = seafloor_ops.shape[0]
    freq = seafloor_ops.shape[1]
    px_dev = seafloor_ops.shape[3]
    py_dev = seafloor_ops.shape[4]
    cols = column_freq.shape[0]
    quad_weight = 2.0 * sens / (px_dev * lax.axis_size("wide") * py_dev * lax.axis_size("narrow"))
    ops_flat = seafloor_ops.reshape(sens, freq * 2, px_dev * py_dev)
    all_cols = lax.all_gather(sensor_data, "narrow", axis=3, tiled=True)
    stored = lax.all_gather(all_cols, "wide", axis=0, tiled=True)
    sensor_rows = jnp.take(stored, row_owner, axis=0)
    freq_mask = (column_freq[None, :] == jnp.arange(freq, dtype=jnp.int32)[:, None]).astype(
        jnp.bfloat16
    )
    probes = (sensor_rows * freq_mask[None, :, None, :]).reshape(sens, freq * 2, cols)
    adjoint = lax.dot_general(
        probes, ops_flat, (((0, 1), (0, 1)), ((), ())), preferred_element_type=jnp.float32
    )
    field = adjoint.reshape(cols, px_dev, py_dev)
    classes = jnp.arange(coef_table.shape[0], dtype=jnp.int32)
    picks = (coef_class[None, :, :] == classes[:, None, None]).astype(jnp.float32)
    kappa = jnp.sum(picks * coef_table[:, None, None], axis=0)
    kappa_pad = extended(kappa, (("wide", 0), ("narrow", 1)), 1)
    for turn in range(SWEEPS):
        padded = extended(field, (("wide", 1), ("narrow", 2)), 1)
        field = sweep(padded, kappa_pad)
    prior_field = field.astype(jnp.bfloat16)
    prior_flat = prior_field.reshape(cols, px_dev * py_dev)
    inverse = jnp.zeros((sens,), jnp.int32).at[row_owner].set(jnp.arange(sens, dtype=jnp.int32))
    partial_value = lax.dot_general(
        ops_flat, prior_flat, (((2,), (1,)), ((), ())), preferred_element_type=jnp.float32
    )
    stored_terms = jnp.take(partial_value * quad_weight, inverse, axis=0).reshape(
        sens, freq, 2, cols
    )
    col_share = lax.psum_scatter(stored_terms, "narrow", scatter_dimension=3, tiled=True)
    hessian = lax.psum_scatter(col_share, "wide", scatter_dimension=0, tiled=True)
    return (hessian.astype(jnp.bfloat16), prior_field)


def solution(mesh):
    placed = (
        P(None, None, None, "wide", "narrow"),
        P("wide", None, None, "narrow"),
        P(),
        P(),
        P("wide", "narrow"),
        P(),
    )
    return jax.shard_map(
        on_device,
        mesh=mesh,
        in_specs=placed,
        out_specs=(P("wide", None, None, "narrow"), P(None, "wide", "narrow")),
        check_vma=False,
    )
```

profile of v0, /device:TPU:0, one launch (start us, length us, event | category | flops | bytes accessed | tf_op | source)
XLA Modules:
  0.0 377.9 jit_solution(12119162614868587440)
XLA Ops:
  7.2 0.8 copy.39
  8.0 27.1 %all_gather.6 = bf16[64,4,2,256]{0,1,2,3:T(4,128)(2,1)S(1)} all-gather(bf16[64,4,2,16]{0,1,2,3:T(4,128)(2,1)S(1)} %copy.39), channel_id=1, replica_groups=mesh['wide'=8,'narrow'=16] {'narrow'}, dimensions={3}, use_global_device_ids=true | all-gather | bytes 278528 | tf_op jit(solution)/shard_map/all_gather | solution.py:40
  35.1 1.1 copy.40
  36.3 0.8 select_reduce_fusion
  37.1 1.3 collective-permute-start
  38.4 4.5 %collective-permute-start.2 = (f32[1,128]{1,0:T(1,128)S(1)}, f32[1,128]{1,0:T(1,128)S(1)}, u32[]{:S(2)}, u32[]{:S(2)}) collective-permute-start(f32[1,128]{1,0:T(1,128)S(1)} %get-tuple-element.30), channel_id=1, source_target_pairs={{0,16},{16,32},{32,48},{48,64},{64,80},{80,96},{96,112},{1,17},{17... | collective-permute-start | bytes 1544 | tf_op jit(solution)/shard_map/ppermute | solution.py:16
  43.0 0.7 compare_and_fusion
  43.7 0.7 fusion.50
  44.3 0.7 compare_select_fusion.1
  45.0 25.4 %reshape.104 = bf16[512,8,2048]{2,1,0:T(8,128)(2,1)} reshape(bf16[512,4,2,16,128]{4,3,2,1,0:T(8,128)(2,1)} %param.6) | data formatting | bytes 33554432 | tf_op jit(solution)/shard_map/reshape | solution.py:39
  70.4 25.6 %copy.51 = bf16[512,8,2048]{0,1,2:T(8,128)(2,1)} copy(bf16[512,8,2048]{2,1,0:T(8,128)(2,1)} %reshape.104) | data formatting | bytes 33554432 | tf_op jit(solution)/shard_map/reshape | solution.py:39
  96.0 4.2 %gather_fusion = bf16[512,4,2,256]{3,1,2,0:T(4,128)(2,1)S(1)} fusion(bf16[512,4,2,256]{3,1,2,0:T(4,128)(2,1)} %all-gather.2.cloned.1.call-done, s32[1024]{0:T(1024)S(1)} %pad_clamp_fusion.1), kind=kCustom, calls=%fused_computation | custom fusion | bytes 4196352 | tf_op jit(solution)/shard_map/jit(_take)/gather | solution.py:42
  100.2 2.0 select_multiply_fusion
  102.2 1.7 copy.41
  104.0 20.0 %fusion.43 = f32[256,16,128]{0,2,1:T(8,128)S(1)} fusion(bf16[512,8,256,1]{2,0,1,3:T(8,128)(2,1)} %bitcast.26, bf16[16,128,512,8]{2,3,1,0:T(8,128)(2,1)} %bitcast.23), kind=kOutput, calls=%fused_computation.71 | convolution fusion | flops 4294967296 | bytes 20971520 | tf_op jit(solution)/shard_map/dot_general | solution.py:47
  124.0 1.3 collective-permute-start.1
  125.3 4.6 %collective-permute-start.3 = (f32[256,1,128]{0,2,1:T(8,128)S(1)}, f32[256,1,128]{0,2,1:T(8,128)S(1)}, u32[]{:S(2)}, u32[]{:S(2)}) collective-permute-start(f32[256,1,128]{0,2,1:T(8,128)S(1)} %get-tuple-element.22), channel_id=1, source_target_pairs={{0,16},{16,32},{32,48},{48,64},{64,80},{80,96},{96,112},{1,17},{17... | collective-permute-start | bytes 393224 | tf_op jit(solution)/shard_map/ppermute | solution.py:16
  129.9 1.3 collective-permute-start.4
  131.2 3.0 collective-permute-start.6
  134.3 3.9 %collective-permute-start.7 = (f32[256,18,1]{0,2,1:T(1,128)S(1)}, f32[256,18,1]{0,2,1:T(1,128)S(1)}, u32[]{:S(2)}, u32[]{:S(2)}) collective-permute-start(f32[256,18,1]{0,2,1:T(1,128)S(1)} %get-tuple-element.17), channel_id=1, source_target_pairs={{0,1},{1,2},{2,3},{3,4},{4,5},{5,6},{6,7},{7,8},{8,9},{9,10},{10,1... | collective-permute-start | bytes 55304 | tf_op jit(solution)/shard_map/ppermute | solution.py:16
  138.2 1.3 collective-permute-start.5
  139.6 1.7 collective-permute-done.5
  141.3 6.9 %fusion.32 = f32[256,16,128]{0,2,1:T(8,128)S(1)} fusion(f32[256,16,128]{0,2,1:T(8,128)} %copy-done, f32[256,18,1]{0,2,1:T(1,128)S(1)} %collective-permute-done.7, f32[256,1,128]{0,2,1:T(8,128)S(1)} %collective-permute-done.1, f32[256,1,128]{0,2,1:T(8,128)S(1)} %collective-permute-done.3, f32[256,18,1]{0,2,1:T(1,128)S(1)} %collective-permute-done.5, ...), kind=kLoop, calls=%fused_computation.53 | loop fusion | flops 10485760 | bytes 4526080 | tf_op jit(solution)/shard_map/add | solution.py:29
  148.2 1.3 collective-permute-start.8
  149.5 4.6 %collective-permute-start.9 = (f32[256,1,128]{0,2,1:T(8,128)S(1)}, f32[256,1,128]{0,2,1:T(8,128)S(1)}, u32[]{:S(2)}, u32[]{:S(2)}) collective-permute-start(f32[256,1,128]{0,2,1:T(8,128)S(1)} %get-tuple-element.20), channel_id=1, source_target_pairs={{0,16},{16,32},{32,48},{48,64},{64,80},{80,96},{96,112},{1,17},{17... | collective-permute-start | bytes 393224 | tf_op jit(solution)/shard_map/ppermute | solution.py:16
  154.1 2.4 scatter_custom_fusion
  156.6 4.8 %collective-permute-start.11 = (f32[256,18,1]{0,2,1:T(1,128)S(1)}, f32[256,18,1]{0,2,1:T(1,128)S(1)}, u32[]{:S(2)}, u32[]{:S(2)}) collective-permute-start(f32[256,18,1]{0,2,1:T(1,128)S(1)} %get-tuple-element.15), channel_id=1, source_target_pairs={{0,1},{1,2},{2,3},{3,4},{4,5},{5,6},{6,7},{7,8},{8,9},{9,10},{10,1... | collective-permute-start | bytes 55304 | tf_op jit(solution)/shard_map/ppermute | solution.py:16
  161.5 1.3 collective-permute-start.10
  162.8 3.1 collective-permute-done.10
  165.9 2.3 fusion.20
  168.3 1.3 collective-permute-start.12
  169.6 5.0 %collective-permute-start.13 = (f32[256,1,128]{0,2,1:T(8,128)S(1)}, f32[256,1,128]{0,2,1:T(8,128)S(1)}, u32[]{:S(2)}, u32[]{:S(2)}) collective-permute-start(f32[256,1,128]{0,2,1:T(8,128)S(1)} %get-tuple-element.18), channel_id=1, source_target_pairs={{0,16},{16,32},{32,48},{48,64},{64,80},{80,96},{96,112},{1,17},{17... | collective-permute-start | bytes 393224 | tf_op jit(solution)/shard_map/ppermute | solution.py:16
  174.6 1.0 collective-permute-done.12
  175.6 1.5 collective-permute-done.13
  177.1 5.1 %collective-permute-start.15 = (f32[256,18,1]{0,2,1:T(1,128)S(1)}, f32[256,18,1]{0,2,1:T(1,128)S(1)}, u32[]{:S(2)}, u32[]{:S(2)}) collective-permute-start(f32[256,18,1]{0,2,1:T(1,128)S(1)} %get-tuple-element.13), channel_id=1, source_target_pairs={{0,1},{1,2},{2,3},{3,4},{4,5},{5,6},{6,7},{7,8},{8,9},{9,10},{10,1... | collective-permute-start | bytes 55304 | tf_op jit(solution)/shard_map/ppermute | solution.py:16
  182.2 1.3 collective-permute-start.14
  183.5 2.3 collective-permute-done.14
  185.8 2.6 fusion.8
  188.4 27.6 %multiply_bitcast_fusion = f32[512,8,256]{0,2,1:T(8,128)} fusion(bf16[256,2048,1]{0,1,2:T(8,128)(2,1)S(1)} %bitcast.25, bf16[512,8,2048]{2,1,0:T(8,128)(2,1)} %reshape.104), kind=kOutput, calls=%fused_computation.7 | convolution fusion | flops 4296015872 | bytes 22020096 | tf_op jit(solution)/shard_map/dot_general | solution.py:61
  216.0 5.4 %copy.46 = f32[512,8,256]{2,1,0:T(8,128)} copy(f32[512,8,256]{0,2,1:T(8,128)} %multiply_bitcast_fusion) | data formatting | bytes 8388608 | tf_op jit(solution)/shard_map/mul | solution.py:64
  221.4 5.2 %gather_fusion.1 = f32[512,8,256]{2,1,0:T(8,128)} fusion(f32[512,8,256]{2,1,0:T(8,128)} %copy.46, s32[1024]{0:T(1024)S(1)} %pad_clamp_fusion), kind=kCustom, calls=%fused_computation.1 | custom fusion | bytes 8390656 | tf_op jit(solution)/shard_map/jit(_take)/gather | solution.py:64
  226.6 5.3 %copy.54 = f32[512,8,256]{0,2,1:T(8,128)} copy(f32[512,8,256]{2,1,0:T(8,128)} %gather_fusion.1) | data formatting | bytes 8388608 | tf_op jit(solution)/shard_map/jit(_take)/gather | solution.py:64
  231.9 4.9 %broadcast_select_fusion = f32[512,4,2,256]{0,3,2,1:T(8,128)} fusion(f32[512,4,2,256]{0,3,2,1:T(8,128)} %bitcast.24, pred[512]{0:T(512)(128)(4,1)S(1)} %compare_and_fusion.1), kind=kLoop, calls=%fused_computation.69 | loop fusion | flops 1048576 | bytes 8389120 | tf_op jit(solution)/shard_map/jit(_take)/select_n | solution.py:64
  236.9 93.9 %reduce-scatter.5.cloned.1.call-done = f32[512,4,2,16]{0,3,2,1:T(8,128)} async-done(((f32[512,4,2,256]{0,3,2,1:T(8,128)}), f32[512,4,2,16]{0,3,2,1:T(8,128)}) %reduce-scatter.5.cloned.1.call-update) | async-done | bytes 262160 | tf_op jit(solution)/shard_map/reduce_scatter | solution.py:67
  330.8 1.8 copy.57
  332.6 1.8 copy.48
  334.4 35.1 %reduce-scatter.7.cloned.1.call-done = f32[64,128]{1,0:T(8,128)} async-done(((f32[512,128]{1,0:T(8,128)}), f32[64,128]{1,0:T(8,128)}) %reduce-scatter.7.cloned.1.call-update) | async-done | bytes 32784
  369.5 1.5 copy.58
  (35 shorter events, 0.6 us)
Async XLA Ops:
  7.2 88.8 %all-gather.2.cloned.1.call-start = ((), (), s32[]{:S(2)}) async-start(), calls=%async_computation.2 | async-start | bytes 2359296 | tf_op jit(solution)/shard_map/all_gather | solution.py:41
  36.3 294.5 %reduce-scatter.5.cloned.1.call-start = ((), (), s32[]{:S(2)}) async-start(), calls=%async_computation.3 | async-start | bytes 4456448 | tf_op jit(solution)/shard_map/reduce_scatter | solution.py:67
  37.1 58.9 %collective-permute-start = (f32[1,128]{1,0:T(1,128)S(1)}, f32[1,128]{1,0:T(1,128)S(1)}, u32[]{:S(2)}, u32[]{:S(2)}) collective-permute-start(f32[1,128]{1,0:T(1,128)S(1)} %get-tuple-element.31), channel_id=1, source_target_pairs={{16,0},{32,16},{48,32},{64,48},{80,64},{96,80},{112,96},{17,1},{33... | collective-permute-start | bytes 1544 | tf_op jit(solution)/shard_map/ppermute | solution.py:17
  38.4 57.6 %collective-permute-start.2 = (f32[1,128]{1,0:T(1,128)S(1)}, f32[1,128]{1,0:T(1,128)S(1)}, u32[]{:S(2)}, u32[]{:S(2)}) collective-permute-start(f32[1,128]{1,0:T(1,128)S(1)} %get-tuple-element.30), channel_id=1, source_target_pairs={{0,16},{16,32},{32,48},{48,64},{64,80},{80,96},{96,112},{1,17},{17... | collective-permute-start | bytes 1544 | tf_op jit(solution)/shard_map/ppermute | solution.py:16
  124.0 17.4 %copy-start = (f32[256,16,128]{0,2,1:T(8,128)}, f32[256,16,128]{0,2,1:T(8,128)S(1)}, u32[]{:S(2)}) copy-start(f32[256,16,128]{0,2,1:T(8,128)S(1)} %fusion.43) | copy-start | bytes 6291460
  124.0 10.3 %collective-permute-start.1 = (f32[256,1,128]{0,2,1:T(8,128)S(1)}, f32[256,1,128]{0,2,1:T(8,128)S(1)}, u32[]{:S(2)}, u32[]{:S(2)}) collective-permute-start(f32[256,1,128]{0,2,1:T(8,128)S(1)} %get-tuple-element.23), channel_id=1, source_target_pairs={{16,0},{32,16},{48,32},{64,48},{80,64},{96,80},{112,96},{17,1},{33... | collective-permute-start | bytes 393224 | tf_op jit(solution)/shard_map/ppermute | solution.py:17
  125.3 9.0 %collective-permute-start.3 = (f32[256,1,128]{0,2,1:T(8,128)S(1)}, f32[256,1,128]{0,2,1:T(8,128)S(1)}, u32[]{:S(2)}, u32[]{:S(2)}) collective-permute-start(f32[256,1,128]{0,2,1:T(8,128)S(1)} %get-tuple-element.22), channel_id=1, source_target_pairs={{0,16},{16,32},{32,48},{48,64},{64,80},{80,96},{96,112},{1,17},{17... | collective-permute-start | bytes 393224 | tf_op jit(solution)/shard_map/ppermute | solution.py:16
  129.9 9.6 %collective-permute-start.4 = (f32[18,1]{1,0:T(8,128)S(1)}, f32[18,1]{1,0:T(8,128)S(1)}, u32[]{:S(2)}, u32[]{:S(2)}) collective-permute-start(f32[18,1]{1,0:T(8,128)S(1)} %get-tuple-element.24), channel_id=1, source_target_pairs={{1,0},{2,1},{3,2},{4,3},{5,4},{6,5},{7,6},{8,7},{9,8},{10,9},{11,1... | collective-permute-start | bytes 224 | tf_op jit(solution)/shard_map/ppermute | solution.py:17
  131.2 8.3 %collective-permute-start.6 = (f32[18,1]{1,0:T(8,128)S(1)}, f32[18,1]{1,0:T(8,128)S(1)}, u32[]{:S(2)}, u32[]{:S(2)}) collective-permute-start(f32[18,1]{1,0:T(8,128)S(1)} %get-tuple-element.25), channel_id=1, source_target_pairs={{0,1},{1,2},{2,3},{3,4},{4,5},{5,6},{6,7},{7,8},{8,9},{9,10},{10,1... | collective-permute-start | bytes 224 | tf_op jit(solution)/shard_map/ppermute | solution.py:16
  134.3 5.3 %collective-permute-start.7 = (f32[256,18,1]{0,2,1:T(1,128)S(1)}, f32[256,18,1]{0,2,1:T(1,128)S(1)}, u32[]{:S(2)}, u32[]{:S(2)}) collective-permute-start(f32[256,18,1]{0,2,1:T(1,128)S(1)} %get-tuple-element.17), channel_id=1, source_target_pairs={{0,1},{1,2},{2,3},{3,4},{4,5},{5,6},{6,7},{7,8},{8,9},{9,10},{10,1... | collective-permute-start | bytes 55304 | tf_op jit(solution)/shard_map/ppermute | solution.py:16
  138.2 3.1 collective-permute-start.5
  148.2 8.3 %collective-permute-start.8 = (f32[256,1,128]{0,2,1:T(8,128)S(1)}, f32[256,1,128]{0,2,1:T(8,128)S(1)}, u32[]{:S(2)}, u32[]{:S(2)}) collective-permute-start(f32[256,1,128]{0,2,1:T(8,128)S(1)} %get-tuple-element.21), channel_id=1, source_target_pairs={{16,0},{32,16},{48,32},{64,48},{80,64},{96,80},{112,96},{17,1},{33... | collective-permute-start | bytes 393224 | tf_op jit(solution)/shard_map/ppermute | solution.py:17
  149.5 7.1 %collective-permute-start.9 = (f32[256,1,128]{0,2,1:T(8,128)S(1)}, f32[256,1,128]{0,2,1:T(8,128)S(1)}, u32[]{:S(2)}, u32[]{:S(2)}) collective-permute-start(f32[256,1,128]{0,2,1:T(8,128)S(1)} %get-tuple-element.20), channel_id=1, source_target_pairs={{0,16},{16,32},{32,48},{48,64},{64,80},{80,96},{96,112},{1,17},{17... | collective-permute-start | bytes 393224 | tf_op jit(solution)/shard_map/ppermute | solution.py:16
  156.6 6.2 %collective-permute-start.11 = (f32[256,18,1]{0,2,1:T(1,128)S(1)}, f32[256,18,1]{0,2,1:T(1,128)S(1)}, u32[]{:S(2)}, u32[]{:S(2)}) collective-permute-start(f32[256,18,1]{0,2,1:T(1,128)S(1)} %get-tuple-element.15), channel_id=1, source_target_pairs={{0,1},{1,2},{2,3},{3,4},{4,5},{5,6},{6,7},{7,8},{8,9},{9,10},{10,1... | collective-permute-start | bytes 55304 | tf_op jit(solution)/shard_map/ppermute | solution.py:16
  161.5 4.4 %collective-permute-start.10 = (f32[256,18,1]{0,2,1:T(1,128)S(1)}, f32[256,18,1]{0,2,1:T(1,128)S(1)}, u32[]{:S(2)}, u32[]{:S(2)}) collective-permute-start(f32[256,18,1]{0,2,1:T(1,128)S(1)} %get-tuple-element.14), channel_id=1, source_target_pairs={{1,0},{2,1},{3,2},{4,3},{5,4},{6,5},{7,6},{8,7},{9,8},{10,9},{11,1... | collective-permute-start | bytes 55304 | tf_op jit(solution)/shard_map/ppermute | solution.py:17
  168.3 7.3 %collective-permute-start.12 = (f32[256,1,128]{0,2,1:T(8,128)S(1)}, f32[256,1,128]{0,2,1:T(8,128)S(1)}, u32[]{:S(2)}, u32[]{:S(2)}) collective-permute-start(f32[256,1,128]{0,2,1:T(8,128)S(1)} %get-tuple-element.19), channel_id=1, source_target_pairs={{16,0},{32,16},{48,32},{64,48},{80,64},{96,80},{112,96},{17,1},{33... | collective-permute-start | bytes 393224 | tf_op jit(solution)/shard_map/ppermute | solution.py:17
  169.6 7.5 %collective-permute-start.13 = (f32[256,1,128]{0,2,1:T(8,128)S(1)}, f32[256,1,128]{0,2,1:T(8,128)S(1)}, u32[]{:S(2)}, u32[]{:S(2)}) collective-permute-start(f32[256,1,128]{0,2,1:T(8,128)S(1)} %get-tuple-element.18), channel_id=1, source_target_pairs={{0,16},{16,32},{32,48},{48,64},{64,80},{80,96},{96,112},{1,17},{17... | collective-permute-start | bytes 393224 | tf_op jit(solution)/shard_map/ppermute | solution.py:16
  177.1 6.4 %collective-permute-start.15 = (f32[256,18,1]{0,2,1:T(1,128)S(1)}, f32[256,18,1]{0,2,1:T(1,128)S(1)}, u32[]{:S(2)}, u32[]{:S(2)}) collective-permute-start(f32[256,18,1]{0,2,1:T(1,128)S(1)} %get-tuple-element.13), channel_id=1, source_target_pairs={{0,1},{1,2},{2,3},{3,4},{4,5},{5,6},{6,7},{7,8},{8,9},{9,10},{10,1... | collective-permute-start | bytes 55304 | tf_op jit(solution)/shard_map/ppermute | solution.py:16
  182.2 3.6 collective-permute-start.14
  236.8 132.7 %reduce-scatter.7.cloned.1.call-start = ((), (), s32[]{:S(2)}) async-start(), calls=%async_computation.4 | async-start | bytes 294912
Sparse Core Ops, SparseCore 0:
  36.4 37.6 all-gather.1
  236.9 93.8 reduce-scatter.4
  333.1 36.3 reduce-scatter.6
where the time goes:
time: 384 us; the launch traced here: 378 us
  waiting for transfers between devices  139 us (36%)
  local copies, waits for them, and re-layouts  82.3 us (21%)
  matrix products  47.6 us (12%)
  starting transfers between devices  46 us (12%)
  blocking collectives  27.1 us (7%)
  other arithmetic  21.8 us (6%)
  between operations  14.5 us (4%)
    reduce_scatter x1, waiting for transfers between devices, on_device(): lax.psum_scatter(stored_terms, 'narrow', scatter_dimension=3, tiled=True)  93.9 us
    reshape x2, local copies, waits for them, and re-layouts, on_device(): ops_flat = seafloor_ops.reshape(sens, freq * 2, px_dev * py_dev)  50.9 us
    ppermute x8, starting transfers between devices, extended(): before = lax.ppermute(last, axis, up)  35.5 us
    unnamed x4, waiting for transfers between devices  35.2 us
    dot_general x1, matrix products, on_device(): lax.dot_general(ops_flat, prior_flat, (((2,), (1,)), ((), ())), preferred...  27.6 us
    all_gather x1, blocking collectives, on_device(): all_cols = lax.all_gather(sensor_data, 'narrow', axis=3, tiled=True)  27.1 us
    dot_general x1, matrix products, on_device(): lax.dot_general(probes, ops_flat, (((0, 1), (0, 1)), ((), ())), preferred...  20 us
    gather x2, local copies, waits for them, and re-layouts, on_device(): jnp.take(partial_value * quad_weight, inverse, axis=0)  10.4 us
  transfers between devices with their start and end apart: 19, of which 7 were waited for; matrix products, arithmetic and copies ran while one was open for 15% of the time, Pallas kernels for 0%

commit v1 on v0

v1 whole, which is shorter than its diff:
```python
import jax
import jax.numpy as jnp
from jax import lax
from jax.experimental import pallas as pl
from jax.experimental.pallas import tpu as pltpu
from jax.sharding import PartitionSpec as P

SWEEPS = 3
BOTH = ("wide", "narrow")
F32 = jnp.float32
BF16 = jnp.bfloat16
WHOLE = pl.BlockSpec(memory_space=pltpu.VMEM)
SCALARS = pl.BlockSpec(memory_space=pltpu.SMEM)
PX, PY = 16, 128
COLS, FREQ, NW, KW = 256, 4, 8, 512
STRIP = 24


def params(mib):
    return pltpu.CompilerParams(vmem_limit_bytes=mib << 20)


def relayout_body(inv, ops, out, buf, sems):
    group = pl.program_id(0)
    per = buf.shape[2]

    def fetch(which, slot):
        def one(j, _):
            sensor = inv[which * per + j]
            pltpu.make_async_copy(ops.at[sensor], buf.at[slot, :, j], sems.at[slot]).start()
            return 0

        lax.fori_loop(0, per, one, 0, unroll=8)

    @pl.when(group == 0)
    def _():
        fetch(0, 0)

    @pl.when(group + 1 < pl.num_programs(0))
    def _():
        fetch(group + 1, (group + 1) % 2)

    slot = group % 2
    pltpu.make_async_copy(buf.at[slot], buf.at[slot], sems.at[slot]).wait()
    for f in range(FREQ):
        block = buf[slot, f].reshape(per * 2, PX, PY)
        start = pl.multiple_of(group * KW + f * per * 2, per * 2)
        out[:, pl.ds(start, per * 2), :] = jnp.swapaxes(block, 0, 1)


def relayout(ops, inv):
    sens = ops.shape[0]
    per = sens // NW
    return pl.pallas_call(
        relayout_body,
        grid=(NW,),
        in_specs=[SCALARS, pl.BlockSpec(memory_space=pl.ANY)],
        out_specs=WHOLE,
        out_shape=jax.ShapeDtypeStruct((PX, sens * FREQ * 2, PY), BF16),
        scratch_shapes=[
            pltpu.VMEM((2, FREQ, per, 2, PX, PY), BF16),
            pltpu.SemaphoreType.DMA((2,)),
        ],
        compiler_params=params(30),
    )(inv, ops)


def strip_lane(rows):
    left = (rows >= 3) & (rows < 12)
    right = (rows >= 12) & (rows < 21)
    return jnp.where(left, rows - 3, jnp.where(right, rows + (PY - 21), -1))


def adjoint_body(gathered, freq, ops, classes, field, strips, y_up, y_down, probes):
    step = pl.program_id(0)

    @pl.when(step == 0)
    def _():
        for w in range(NW):
            for f in range(FREQ):
                at = w * KW + f * 128
                mine = freq[...] == f
                probes[:, at : at + 128] = jnp.where(mine, gathered[w], 0).astype(BF16)

    pair = jnp.concatenate([ops[2 * step], ops[2 * step + 1]], axis=1)
    both = jnp.dot(probes[...], pair, preferred_element_type=F32)
    rows = lax.broadcasted_iota(jnp.int32, (STRIP, PY), 0)
    lanes = lax.broadcasted_iota(jnp.int32, (STRIP, PY), 1)
    pick = (strip_lane(rows) == lanes).astype(F32)
    nt = (((1,), (1,)), ((), ()))
    for h in range(2):
        x = 2 * step + h
        mine = both[:, h * PY : (h + 1) * PY]
        field[x] = mine
        strip = lax.dot_general(pick, mine, nt, precision=lax.Precision.HIGHEST, preferred_element_type=F32)
        row = jnp.broadcast_to(classes[pl.ds(x, 1), :], (PY, PY))
        label = lax.dot_general(pick, row, nt, preferred_element_type=F32)
        parts = (strip[:, :128], strip[:, 128:], label)
        for t in range(3):
            strips[x, t] = parts[t]
        pad = jnp.zeros((7, 128), F32)
        y_up[x] = jnp.concatenate([p[18:21] for p in parts] + [pad], axis=0).astype(BF16)
        y_down[x] = jnp.concatenate([p[3:6] for p in parts] + [pad], axis=0).astype(BF16)


def adjoint(gathered, freq, ops, classes):
    edge = jax.ShapeDtypeStruct((PX, 16, 128), BF16)
    edge_spec = pl.BlockSpec((PX, 16, 128), lambda i: (0, 0, 0))
    return pl.pallas_call(
        adjoint_body,
        grid=(PX // 2,),
        in_specs=[WHOLE] * 4,
        out_specs=(WHOLE, WHOLE, edge_spec, edge_spec),
        out_shape=(
            jax.ShapeDtypeStruct((PX, COLS, PY), F32),
            jax.ShapeDtypeStruct((PX, 3, STRIP, 128), F32),
            edge,
            edge,
        ),
        scratch_shapes=[pltpu.VMEM((COLS, NW * KW), BF16)],
        compiler_params=params(30),
    )(gathered, freq, ops, classes)


XROWS = COLS + 16 + 3 * STRIP


def edges_body(field, strips, before, after, classes, whole_strips, x_up, x_down):
    for x in range(PX):
        for t in range(3):
            low = before[x].astype(F32)[3 * t : 3 * t + 3]
            high = after[x].astype(F32)[3 * t : 3 * t + 3]
            whole_strips[x, t] = jnp.concatenate([low, strips[x, t, 3:21, :], high], axis=0)
    for first, out in ((PX - 3, x_up), (0, x_down)):
        for j in range(3):
            x = first + j
            out[j, :COLS] = field[x].astype(BF16)
            out[j, COLS : COLS + 16] = jnp.broadcast_to(classes[x : x + 1, :], (16, PY)).astype(BF16)
            for t in range(3):
                at = COLS + 16 + t * STRIP
                out[j, at : at + STRIP] = whole_strips[x, t].astype(BF16)


def edges(field, strips, before, after, classes):
    send = jax.ShapeDtypeStruct((3, XROWS, 128), BF16)
    return pl.pallas_call(
        edges_body,
        in_specs=[WHOLE] * 5,
        out_specs=(WHOLE, pl.BlockSpec(), pl.BlockSpec()),
        out_shape=(jax.ShapeDtypeStruct((PX, 3, STRIP, 128), F32), send, send),
        compiler_params=params(30),
    )(field, strips, before, after, classes)


def table_of(labels, table):
    kappa = jnp.zeros(labels.shape, F32)
    for j in range(8):
        kappa = jnp.where(labels == float(j + 1), table[j], kappa)
    return kappa


def weights(here, up, down, left, right):
    four = [jnp.minimum(here, n) for n in (up, down, left, right)]
    return [1.0 - (four[0] + four[1] + four[2] + four[3])] + four


def smooth(value, load, axis, size):
    for turn in range(SWEEPS):
        fresh = []
        for i in range(1, len(value) - 1):
            m = load(i + turn)
            mid = value[i]
            left = pltpu.roll(mid, 1, axis)
            right = pltpu.roll(mid, size - 1, axis)
            a = m[0] * mid + m[1] * value[i - 1]
            b = m[2] * value[i + 1] + m[3] * left
            fresh.append(a + (b + m[4] * right))
        value = fresh
    return value


def sweep_body(table, field, strips, above, below, classes, prior, prior_out, main_w, strip_w):
    ext = PX + 6
    label = [above[j, COLS : COLS + 8].astype(F32) for j in range(3)]
    label += [jnp.broadcast_to(classes[x : x + 1, :], (8, PY)) for x in range(PX)]
    label += [below[j, COLS : COLS + 8].astype(F32) for j in range(3)]
    kappa = [table_of(v, table) for v in label]
    for i in range(1, ext - 1):
        k = kappa[i]
        ws = weights(k, kappa[i - 1], kappa[i + 1], pltpu.roll(k, 1, 1), pltpu.roll(k, PY - 1, 1))
        for d in range(5):
            main_w[i, d] = ws[d]
    at = COLS + 16

    def strip_rows(t):
        lo, hi = at + t * STRIP, at + (t + 1) * STRIP
        return (
            [above[j, lo:hi].astype(F32) for j in range(3)]
            + [strips[x, t] for x in range(PX)]
            + [below[j, lo:hi].astype(F32) for j in range(3)]
        )

    kappa = [table_of(v, table) for v in strip_rows(2)]
    for i in range(1, ext - 1):
        k = kappa[i]
        ws = weights(k, kappa[i - 1], kappa[i + 1], pltpu.roll(k, 1, 0), pltpu.roll(k, STRIP - 1, 0))
        for d in range(5):
            strip_w[i, d] = ws[d]
    edge = [smooth(strip_rows(t), lambda i: [strip_w[i, d] for d in range(5)], 0, STRIP) for t in range(2)]
    rows = lax.broadcasted_iota(jnp.int32, (STRIP, PY), 0)
    lanes = lax.broadcasted_iota(jnp.int32, (STRIP, PY), 1)
    pick = (strip_lane(rows) == lanes).astype(BF16)
    tn = (((0,), (0,)), ((), ()))
    for x in range(PX):
        both = jnp.concatenate([edge[0][x], edge[1][x]], axis=1).astype(BF16)
        prior[x] = lax.dot_general(both, pick, tn, preferred_element_type=F32).astype(BF16)

    def columns(g, _):
        c = pl.multiple_of(g * 16, 16)
        value = [above[j, pl.ds(c, 16), :].astype(F32) for j in range(3)]
        value += [field[x, pl.ds(c, 16), :] for x in range(PX)]
        value += [below[j, pl.ds(c, 16), :].astype(F32) for j in range(3)]

        def load(i):
            return [jnp.concatenate([main_w[i, d]] * 2, axis=0) for d in range(5)]

        value = smooth(value, load, 1, PY)
        lane = lax.broadcasted_iota(jnp.int32, (16, PY), 1)
        inner = (lane >= 3) & (lane < PY - 3)
        for x in range(PX):
            at_edge = prior[x, pl.ds(c, 16), :].astype(F32)
            prior[x, pl.ds(c, 16), :] = jnp.where(inner, value[x], at_edge).astype(BF16)
        return 0

    lax.fori_loop(0, COLS // 16, columns, 0)
    prior_out[...] = jnp.swapaxes(prior[...], 0, 1)


def sweeps(table, field, strips, above, below, classes):
    ext = PX + 6
    return pl.pallas_call(
        sweep_body,
        in_specs=[SCALARS] + [WHOLE] * 5,
        out_specs=(WHOLE, pl.BlockSpec()),
        out_shape=(
            jax.ShapeDtypeStruct((PX, COLS, PY), BF16),
            jax.ShapeDtypeStruct((COLS, PX, PY), BF16),
        ),
        scratch_shapes=[pltpu.VMEM((ext, 5, 8, PY), F32), pltpu.VMEM((ext, 5, STRIP, PY), F32)],
        compiler_params=params(30),
    )(table, field, strips, above, below, classes)


def forward_body(prior, ops, out):
    group = pl.program_id(0)
    rows = pl.ds(pl.multiple_of(group * KW, KW), KW)
    left = jnp.concatenate([prior[x] for x in range(PX)], axis=1)
    right = jnp.concatenate([ops[x, rows, :] for x in range(PX)], axis=1)
    nt = (((1,), (1,)), ((), ()))
    out[0] = lax.dot_general(left, right, nt, preferred_element_type=F32).astype(BF16)


def forward(prior, ops):
    return pl.pallas_call(
        forward_body,
        grid=(NW,),
        in_specs=[WHOLE, WHOLE],
        out_specs=pl.BlockSpec((1, COLS, KW), lambda i: (i, 0, 0)),
        out_shape=jax.ShapeDtypeStruct((NW, COLS, KW), BF16),
        compiler_params=params(30),
    )(prior, ops)


def shifted(value, axis, step):
    size = lax.axis_size(axis)
    return lax.ppermute(value, axis, [(i, i + step) for i in range(size) if 0 <= i + step < size])


def on_device(seafloor_ops, sensor_data, column_freq, row_owner, coef_class, coef_table):
    sens = seafloor_ops.shape[0]
    per, own = sensor_data.shape[0], sensor_data.shape[3]
    quad_weight = 2.0 * sens / (PX * lax.axis_size("wide") * PY * lax.axis_size("narrow"))
    my_freq = lax.dynamic_slice_in_dim(column_freq, lax.axis_index("narrow") * own, own)
    mask = my_freq[None, None, None, :] == jnp.arange(FREQ, dtype=jnp.int32)[None, :, None, None]
    chosen = jnp.sum(jnp.where(mask, sensor_data, 0).astype(F32), axis=1).astype(BF16)
    block = chosen.reshape(per * 2, own).T
    sent = jnp.broadcast_to(block[None], (128,) + block.shape)
    gathered = lax.all_to_all(sent, BOTH, 0, 0, tiled=True).reshape(NW, COLS, per * 2)

    ids = jnp.arange(sens, dtype=jnp.int32)
    inverse = jnp.sum(jnp.where(row_owner[None, :] == ids[:, None], ids[None, :], 0), axis=1)
    classes = (coef_class + 1).astype(F32)

    ops = relayout(seafloor_ops, inverse)
    field, strips, y_up, y_down = adjoint(gathered, column_freq.reshape(COLS, 1), ops, classes)
    before = shifted(y_up, "narrow", 1)
    after = shifted(y_down, "narrow", -1)
    strips, x_up, x_down = edges(field, strips, before, after, classes)
    above = shifted(x_up, "wide", 1)
    below = shifted(x_down, "wide", -1)
    prior, prior_field = sweeps(coef_table, field, strips, above, below, classes)
    partial_value = forward(prior, ops)
    pieces = lax.all_to_all(partial_value.reshape(128, own, KW), BOTH, 0, 0, tiled=True)
    total = jnp.sum(pieces.astype(F32), axis=0) * quad_weight
    hessian = total.astype(BF16).reshape(own, FREQ, per, 2).transpose(2, 1, 3, 0)
    return hessian, prior_field


def solution(mesh):
    placed = (
        P(None, None, None, "wide", "narrow"),
        P("wide", None, None, "narrow"),
        P(),
        P(),
        P("wide", "narrow"),
        P(),
    )
    return jax.shard_map(
        on_device,
        mesh=mesh,
        in_specs=placed,
        out_specs=(P("wide", None, None, "narrow"), P(None, "wide", "narrow")),
        check_vma=False,
    )
```

time: 384 us -> 138 us (0.36)
  the two profiles are of different devices: /device:TPU:0 before, /device:TPU:1 now
where the time goes in v1:
time: 138 us; the launch traced here: 137 us
  blocking collectives  41.5 us (30%)
  Pallas kernels  37.5 us (27%)
  starting transfers between devices  23.4 us (17%)
  local copies, waits for them, and re-layouts  20.7 us (15%)
  waiting for transfers between devices  11 us (8%)
  other arithmetic  2.09 us (2%)
    all_to_all x1, blocking collectives, on_device(): lax.all_to_all(partial_value.reshape(128, own, KW), BOTH, 0, 0, tiled=True)  41.5 us
    unnamed x11, local copies, waits for them, and re-layouts  18 us
    pallas_call x1, Pallas kernels, adjoint(): pl.pallas_call(adjoint_body, grid=(PX // 2,), in_specs=[WHOLE] * 4, out_s...  13.1 us
    ppermute x4, starting transfers between devices, shifted(): lax.ppermute(value, axis, [(i, i + step) for i in range(size) if 0 <= i +...  11.9 us
    all_to_all x1, starting transfers between devices, on_device(): lax.all_to_all(sent, BOTH, 0, 0, tiled=True).reshape(NW, COLS, per * 2)  11.5 us
    ppermute x4, waiting for transfers between devices, shifted(): lax.ppermute(value, axis, [(i, i + step) for i in range(size) if 0 <= i +...  11 us
    pallas_call x1, Pallas kernels, relayout(): pl.pallas_call(relayout_body, grid=(NW,), in_specs=[SCALARS, pl.BlockSpec...  10.3 us
    pallas_call x1, Pallas kernels, sweeps(): pl.pallas_call(sweep_body, in_specs=[SCALARS] + [WHOLE] * 5, out_specs=(W...  8.04 us
  transfers between devices with their start and end apart: 5, of which 3 were waited for; matrix products, arithmetic and copies ran while one was open for 1% of the time, Pallas kernels for 7%

profile of v1, /device:TPU:1, one launch (start us, length us, event | category | flops | bytes accessed | tf_op | source)
XLA Modules:
  0.0 136.9 jit_solution(11668458524859936119)
XLA Ops:
  0.6 0.8 dynamic_slice.3
  1.4 0.8 select_reduce_fusion.1
  2.2 0.1 copy.16
  2.3 0.1 copy.17
  2.4 0.9 broadcast_in_dim.37
  3.3 11.5 %all-to-all-start = ((bf16[128,16,128]{2,1,0:T(8,128)(2,1)}), bf16[128,16,128]{2,1,0:T(8,128)(2,1)S(1)}, u32[]{:S(2)}, u32[]{:S(2)}) async-start(bf16[128,16,128]{2,1,0:T(8,128)(2,1)} %broadcast_in_dim.37), calls=%async_computation | async-start | bytes 1048576 | tf_op jit(solution)/shard_map/all_to_all | solution.py:288
  14.8 0.8 copy.18.freq
  15.6 0.9 select_reduce_fusion.inv
  16.5 0.0 copy-start.4
  16.5 10.3 %shard_map.77.ops = bf16[16,4096,128]{2,1,0:T(8,128)(2,1)S(1)} custom-call(s32[512]{0:T(512)S(1)} %select_reduce_fusion.inv, bf16[512,4,2,16,128]{4,3,2,1,0:T(8,128)(2,1)} %ops.1), custom_call_target="tpu_custom_call" | custom-call | tf_op jit(solution)/shard_map/pallas_call | solution.py:54
  26.8 0.0 copy-start
  26.8 5.7 %copy-done = bf16[16,4096,128]{2,1,0:T(8,128)(2,1)} copy-done((bf16[16,4096,128]{2,1,0:T(8,128)(2,1)}, bf16[16,4096,128]{2,1,0:T(8,128)(2,1)S(1)}, u32[]{:S(2)}) %copy-start) | copy-done | bytes 16777240
  32.5 0.0 copy-done.4
  32.5 0.0 all-to-all-done
  32.5 0.0 copy-start.1
  32.5 5.8 %copy-done.1 = bf16[16,4096,128]{2,1,0:T(8,128)(2,1)S(1)} copy-done((bf16[16,4096,128]{2,1,0:T(8,128)(2,1)S(1)}, bf16[16,4096,128]{2,1,0:T(8,128)(2,1)}, u32[]{:S(2)}) %copy-start.1) | copy-done | bytes 16777240
  38.3 13.1 %shard_map.78 = (f32[16,256,128]{2,1,0:T(8,128)S(1)}, f32[16,3,24,128]{3,2,1,0:T(8,128)S(1)}, bf16[16,16,128]{2,1,0:T(8,128)(2,1)S(1)}, bf16[16,16,128]{2,1,0:T(8,128)(2,1)S(1)}) custom-call(bf16[8,256,128]{2,1,0:T(8,128)(2,1)S(1)} %bitcast.10, s32[256,1]{1,0:T(8,128)S(1)} %copy.18.freq, bf16[16,4096,128]{2,1,0:T(8,128)(2,1)S(1)} %copy-done.1, ...), custom_call_target="tpu_custom_call" | custom-call | tf_op jit(solution)/shard_map/pallas_call | solution.py:109
  51.4 0.0 copy-start.3
  51.4 5.6 %collective-permute-start = (bf16[16,16,128]{2,1,0:T(8,128)(2,1)S(1)}, bf16[16,16,128]{2,1,0:T(8,128)(2,1)S(1)}, u32[]{:S(2)}, u32[]{:S(2)}) collective-permute-start(bf16[16,16,128]{2,1,0:T(8,128)(2,1)S(1)} %get-tuple-element.13), channel_id=1, source_target_pairs={{0,1},{1,2},{2,3},{3,4},{4,5},{5,6},{6,7},{7,8},{8,9},{9,10},{10,1... | collective-permute-start | bytes 196616 | tf_op jit(solution)/shard_map/ppermute | solution.py:276
  56.9 1.9 %collective-permute-start.1 = (bf16[16,16,128]{2,1,0:T(8,128)(2,1)S(1)}, bf16[16,16,128]{2,1,0:T(8,128)(2,1)S(1)}, u32[]{:S(2)}, u32[]{:S(2)}) collective-permute-start(bf16[16,16,128]{2,1,0:T(8,128)(2,1)S(1)} %get-tuple-element.14), channel_id=1, source_target_pairs={{1,0},{2,1},{3,2},{4,3},{5,4},{6,5},{7,6},{8,7},{9,8},{10,9},{11,1... | collective-permute-start | bytes 196616 | tf_op jit(solution)/shard_map/ppermute | solution.py:276
  58.9 0.0 collective-permute-done.before
  58.9 5.2 %collective-permute-done.1.after = bf16[16,16,128]{2,1,0:T(8,128)(2,1)S(1)} collective-permute-done((bf16[16,16,128]{2,1,0:T(8,128)(2,1)S(1)}, bf16[16,16,128]{2,1,0:T(8,128)(2,1)S(1)}, u32[]{:S(2)}, u32[]{:S(2)}) %collective-permute-start.1) | collective-permute-done | bytes 65568 | tf_op jit(solution)/shard_map/ppermute | solution.py:276
  64.0 0.1 shard_map.79
  64.2 3.1 %collective-permute-start.2 = (bf16[3,344,128]{2,1,0:T(8,128)(2,1)S(1)}, bf16[3,344,128]{2,1,0:T(8,128)(2,1)S(1)}, u32[]{:S(2)}, u32[]{:S(2)}) collective-permute-start(bf16[3,344,128]{2,1,0:T(8,128)(2,1)S(1)} %get-tuple-element.16), channel_id=1, source_target_pairs={{0,16},{16,32},{32,48},{48,64},{64,80},{80,96},{96,112},{1,17},{17... | collective-permute-start | bytes 792584 | tf_op jit(solution)/shard_map/ppermute | solution.py:276
  67.3 1.3 collective-permute-start.3
  68.6 2.0 %collective-permute-done.2.above = bf16[3,344,128]{2,1,0:T(8,128)(2,1)S(1)} collective-permute-done((bf16[3,344,128]{2,1,0:T(8,128)(2,1)S(1)}, bf16[3,344,128]{2,1,0:T(8,128)(2,1)S(1)}, u32[]{:S(2)}, u32[]{:S(2)}) %collective-permute-start.2) | collective-permute-done | bytes 264224 | tf_op jit(solution)/shard_map/ppermute | solution.py:276
  70.6 3.8 %collective-permute-done.3.below = bf16[3,344,128]{2,1,0:T(8,128)(2,1)S(1)} collective-permute-done((bf16[3,344,128]{2,1,0:T(8,128)(2,1)S(1)}, bf16[3,344,128]{2,1,0:T(8,128)(2,1)S(1)}, u32[]{:S(2)}, u32[]{:S(2)}) %collective-permute-start.3) | collective-permute-done | bytes 264224 | tf_op jit(solution)/shard_map/ppermute | solution.py:276
  74.4 0.0 copy-done.3
  74.4 8.0 %shard_map.80 = (bf16[16,256,128]{2,1,0:T(8,128)(2,1)S(1)}, bf16[256,16,128]{2,1,0:T(8,128)(2,1)}) custom-call(f32[8]{0:T(128)S(1)} %copy-done.3, f32[16,256,128]{2,1,0:T(8,128)S(1)} %get-tuple-element.11.field, f32[16,3,24,128]{3,2,1,0:T(8,128)S(1)} %get-tuple-element.15.strips, bf16[3,344,128]{2,1,0:T(8,128)(2,1)S(1)} %collective-permute-done.2.above, ...), custom_call_target="tpu_custom_call" | custom-call | tf_op jit(solution)/shard_map/pallas_call | solution.py:241
  82.5 0.0 copy-start.2
  82.5 5.8 %copy-done.2 = bf16[16,4096,128]{2,1,0:T(8,128)(2,1)S(1)} copy-done((bf16[16,4096,128]{2,1,0:T(8,128)(2,1)S(1)}, bf16[16,4096,128]{2,1,0:T(8,128)(2,1)}, u32[]{:S(2)}) %copy-start.2) | copy-done | bytes 16777240
  88.2 6.0 %shard_map.81 = bf16[8,256,512]{2,1,0:T(8,128)(2,1)S(1)} custom-call(bf16[16,256,128]{2,1,0:T(8,128)(2,1)S(1)} %get-tuple-element.18.prior, bf16[16,4096,128]{2,1,0:T(8,128)(2,1)S(1)} %copy-done.2), custom_call_target="tpu_custom_call" | custom-call | tf_op jit(solution)/shard_map/pallas_call | solution.py:264
  94.2 41.5 %all_to_all.10 = bf16[128,16,512]{2,1,0:T(8,128)(2,1)S(1)} all-to-all(bf16[128,16,512]{2,1,0:T(8,128)(2,1)S(1)} %bitcast.9), channel_id=1, replica_groups=mesh['wide'=8,'narrow'=16] {'wide','narrow'}, dimensions={0} | all-to-all | bytes 4194304 | tf_op jit(solution)/shard_map/all_to_all | solution.py:303
  135.7 0.4 convert_reduce_fusion
  136.1 0.1 copy.19
  136.2 0.7 copy.20
  (3 shorter events, 0.0 us)
Async XLA Ops:
  3.3 29.2 %all-to-all-start = ((bf16[128,16,128]{2,1,0:T(8,128)(2,1)}), bf16[128,16,128]{2,1,0:T(8,128)(2,1)S(1)}, u32[]{:S(2)}, u32[]{:S(2)}) async-start(bf16[128,16,128]{2,1,0:T(8,128)(2,1)} %broadcast_in_dim.37), calls=%async_computation | async-start | bytes 1048576 | tf_op jit(solution)/shard_map/all_to_all | solution.py:288
  16.5 16.0 %copy-start.4 = (s32[16,128]{1,0:T(8,128)S(1)}, s32[16,128]{1,0:T(8,128)}, u32[]{:S(2)}) copy-start(s32[16,128]{1,0:T(8,128)} %param.10) | copy-start | bytes 24580
  26.8 5.7 %copy-start = (bf16[16,4096,128]{2,1,0:T(8,128)(2,1)}, bf16[16,4096,128]{2,1,0:T(8,128)(2,1)S(1)}, u32[]{:S(2)}) copy-start(bf16[16,4096,128]{2,1,0:T(8,128)(2,1)S(1)} %shard_map.77.ops) | copy-start | bytes 50331652
  32.5 5.8 %copy-start.1 = (bf16[16,4096,128]{2,1,0:T(8,128)(2,1)S(1)}, bf16[16,4096,128]{2,1,0:T(8,128)(2,1)}, u32[]{:S(2)}) copy-start(bf16[16,4096,128]{2,1,0:T(8,128)(2,1)} %copy-done) | copy-start | bytes 50331652
  51.4 23.1 %copy-start.3 = (f32[8]{0:T(128)S(1)}, f32[8]{0:T(128)}, u32[]{:S(2)}) copy-start(f32[8]{0:T(128)} %table.1) | copy-start | bytes 100
  51.4 7.5 %collective-permute-start = (bf16[16,16,128]{2,1,0:T(8,128)(2,1)S(1)}, bf16[16,16,128]{2,1,0:T(8,128)(2,1)S(1)}, u32[]{:S(2)}, u32[]{:S(2)}) collective-permute-start(bf16[16,16,128]{2,1,0:T(8,128)(2,1)S(1)} %get-tuple-element.13), channel_id=1, source_target_pairs={{0,1},{1,2},{2,3},{3,4},{4,5},{5,6},{6,7},{7,8},{8,9},{9,10},{10,1... | collective-permute-start | bytes 196616 | tf_op jit(solution)/shard_map/ppermute | solution.py:276
  56.9 7.1 %collective-permute-start.1 = (bf16[16,16,128]{2,1,0:T(8,128)(2,1)S(1)}, bf16[16,16,128]{2,1,0:T(8,128)(2,1)S(1)}, u32[]{:S(2)}, u32[]{:S(2)}) collective-permute-start(bf16[16,16,128]{2,1,0:T(8,128)(2,1)S(1)} %get-tuple-element.14), channel_id=1, source_target_pairs={{1,0},{2,1},{3,2},{4,3},{5,4},{6,5},{7,6},{8,7},{9,8},{10,9},{11,1... | collective-permute-start | bytes 196616 | tf_op jit(solution)/shard_map/ppermute | solution.py:276
  64.2 6.4 %collective-permute-start.2 = (bf16[3,344,128]{2,1,0:T(8,128)(2,1)S(1)}, bf16[3,344,128]{2,1,0:T(8,128)(2,1)S(1)}, u32[]{:S(2)}, u32[]{:S(2)}) collective-permute-start(bf16[3,344,128]{2,1,0:T(8,128)(2,1)S(1)} %get-tuple-element.16), channel_id=1, source_target_pairs={{0,16},{16,32},{32,48},{48,64},{64,80},{80,96},{96,112},{1,17},{17... | collective-permute-start | bytes 792584 | tf_op jit(solution)/shard_map/ppermute | solution.py:276
  67.3 7.1 %collective-permute-start.3 = (bf16[3,344,128]{2,1,0:T(8,128)(2,1)S(1)}, bf16[3,344,128]{2,1,0:T(8,128)(2,1)S(1)}, u32[]{:S(2)}, u32[]{:S(2)}) collective-permute-start(bf16[3,344,128]{2,1,0:T(8,128)(2,1)S(1)} %get-tuple-element.17), channel_id=1, source_target_pairs={{16,0},{32,16},{48,32},{64,48},{80,64},{96,80},{112,96},{17,1},{33... | collective-permute-start | bytes 792584 | tf_op jit(solution)/shard_map/ppermute | solution.py:276
  82.5 5.8 %copy-start.2 = (bf16[16,4096,128]{2,1,0:T(8,128)(2,1)S(1)}, bf16[16,4096,128]{2,1,0:T(8,128)(2,1)}, u32[]{:S(2)}) copy-start(bf16[16,4096,128]{2,1,0:T(8,128)(2,1)} %copy-done) | copy-start | bytes 50331652

commit v2 on v1

--- a/solution.py
+++ b/solution.py
@@ -6,7 +6,9 @@
 from jax.sharding import PartitionSpec as P
 
 SWEEPS = 3
-BOTH = ("wide", "narrow")
+WIDE, NARROW = ("z_lo", "x"), ("y", "z_hi", "core")
+BOTH = WIDE + NARROW
+CHIPS = WIDE + NARROW[:2]
 F32 = jnp.float32
 BF16 = jnp.bfloat16
 WHOLE = pl.BlockSpec(memory_space=pltpu.VMEM)
@@ -20,106 +22,94 @@
     return pltpu.CompilerParams(vmem_limit_bytes=mib << 20)
 
 
-def relayout_body(inv, ops, out, buf, sems):
-    group = pl.program_id(0)
-    per = buf.shape[2]
-
-    def fetch(which, slot):
-        def one(j, _):
-            sensor = inv[which * per + j]
-            pltpu.make_async_copy(ops.at[sensor], buf.at[slot, :, j], sems.at[slot]).start()
-            return 0
-
-        lax.fori_loop(0, per, one, 0, unroll=8)
-
-    @pl.when(group == 0)
-    def _():
-        fetch(0, 0)
-
-    @pl.when(group + 1 < pl.num_programs(0))
-    def _():
-        fetch(group + 1, (group + 1) % 2)
-
-    slot = group % 2
-    pltpu.make_async_copy(buf.at[slot], buf.at[slot], sems.at[slot]).wait()
-    for f in range(FREQ):
-        block = buf[slot, f].reshape(per * 2, PX, PY)
-        start = pl.multiple_of(group * KW + f * per * 2, per * 2)
-        out[:, pl.ds(start, per * 2), :] = jnp.swapaxes(block, 0, 1)
-
-
-def relayout(ops, inv):
-    sens = ops.shape[0]
-    per = sens // NW
-    return pl.pallas_call(
-        relayout_body,
-        grid=(NW,),
-        in_specs=[SCALARS, pl.BlockSpec(memory_space=pl.ANY)],
-        out_specs=WHOLE,
-        out_shape=jax.ShapeDtypeStruct((PX, sens * FREQ * 2, PY), BF16),
-        scratch_shapes=[
-            pltpu.VMEM((2, FREQ, per, 2, PX, PY), BF16),
-            pltpu.SemaphoreType.DMA((2,)),
-        ],
-        compiler_params=params(30),
-    )(inv, ops)
-
-
 def strip_lane(rows):
     left = (rows >= 3) & (rows < 12)
     right = (rows >= 12) & (rows < 21)
     return jnp.where(left, rows - 3, jnp.where(right, rows + (PY - 21), -1))
 
 
-def adjoint_body(gathered, freq, ops, classes, field, strips, y_up, y_down, probes):
-    step = pl.program_id(0)
-
-    @pl.when(step == 0)
+def adjoint_body(inv, gathered, freq, stored, classes, ops, field, strips, y_up, y_down, buf, sems, probes):
+    group = pl.program_id(0)
+    per = buf.shape[2]
+
+    def fetch(which, slot):
+        def one(j, _):
+            sensor = inv[which * per + j]
+            pltpu.make_async_copy(stored.at[sensor], buf.at[slot, :, j], sems.at[slot]).start()
+            return 0
+
+        lax.fori_loop(0, per, one, 0, unroll=8)
+
+    @pl.when(group == 0)
     def _():
-        for w in range(NW):
-            for f in range(FREQ):
-                at = w * KW + f * 128
-                mine = freq[...] == f
-                probes[:, at : at + 128] = jnp.where(mine, gathered[w], 0).astype(BF16)
-
-    pair = jnp.concatenate([ops[2 * step], ops[2 * step + 1]], axis=1)
-    both = jnp.dot(probes[...], pair, preferred_element_type=F32)
-    rows = lax.broadcasted_iota(jnp.int32, (STRIP, PY), 0)
-    lanes = lax.broadcasted_iota(jnp.int32, (STRIP, PY), 1)
-    pick = (strip_lane(rows) == lanes).astype(F32)
-    nt = (((1,), (1,)), ((), ()))
-    for h in range(2):
-        x = 2 * step + h
-        mine = both[:, h * PY : (h + 1) * PY]
-        field[x] = mine
-        strip = lax.dot_general(pick, mine, nt, precision=lax.Precision.HIGHEST, preferred_element_type=F32)
-        row = jnp.broadcast_to(classes[pl.ds(x, 1), :], (PY, PY))
-        label = lax.dot_general(pick, row, nt, preferred_element_type=F32)
-        parts = (strip[:, :128], strip[:, 128:], label)
-        for t in range(3):
-            strips[x, t] = parts[t]
-        pad = jnp.zeros((7, 128), F32)
-        y_up[x] = jnp.concatenate([p[18:21] for p in parts] + [pad], axis=0).astype(BF16)
-        y_down[x] = jnp.concatenate([p[3:6] for p in parts] + [pad], axis=0).astype(BF16)
-
-
-def adjoint(gathered, freq, ops, classes):
+        fetch(0, 0)
+        field[...] = jnp.zeros_like(field)
+
+    @pl.when(group + 1 < pl.num_programs(0))
+    def _():
+        fetch(group + 1, (group + 1) % 2)
+
+    slot = group % 2
+    block = gathered[group]
+    for f in range(FREQ):
+        probes[:, f * 128 : f * 128 + 128] = jnp.where(freq[...] == f, block, 0).astype(BF16)
+    pltpu.make_async_copy(buf.at[slot], buf.at[slot], sems.at[slot]).wait()
+    rows = pl.ds(pl.multiple_of(group * KW, KW), KW)
+    for f in range(FREQ):
+        start = pl.multiple_of(group * KW + f * per * 2, per * 2)
+        tile = buf[slot, f].reshape(per * 2, PX, PY)
+        ops[:, pl.ds(start, per * 2), :] = jnp.swapaxes(tile, 0, 1)
+    for x in range(0, PX, 2):
+        pair = jnp.concatenate([ops[x, rows, :], ops[x + 1, rows, :]], axis=1)
+        both = jnp.dot(probes[...], pair, preferred_element_type=F32)
+        field[x] += both[:, :PY]
+        field[x + 1] += both[:, PY:]
+
+    @pl.when(group == pl.num_programs(0) - 1)
+    def _():
+        line = lax.broadcasted_iota(jnp.int32, (STRIP, 2 * PY), 0)
+        lanes = lax.broadcasted_iota(jnp.int32, (STRIP, 2 * PY), 1)
+        pick = (strip_lane(line) == lanes % PY).astype(F32).astype(BF16)
+        nt = (((1,), (1,)), ((), ()))
+        for x in range(PX):
+            mine = field[x]
+            high = mine.astype(BF16)
+            low = (mine - high.astype(F32)).astype(BF16)
+            strip = lax.dot_general(pick, jnp.concatenate([high, low], axis=1), nt, preferred_element_type=F32)
+            row = jnp.broadcast_to(classes[x : x + 1, :], (PY, PY)).astype(BF16)
+            label = lax.dot_general(pick[:, :PY], row, nt, preferred_element_type=F32)
+            parts = (strip[:, :128], strip[:, 128:], label)
+            for t in range(3):
+                strips[x, t] = parts[t]
+            pad = jnp.zeros((7, 128), F32)
+            y_up[x] = jnp.concatenate([p[18:21] for p in parts] + [pad], axis=0).astype(BF16)
+            y_down[x] = jnp.concatenate([p[3:6] for p in parts] + [pad], axis=0).astype(BF16)
+
+
+def adjoint(inv, gathered, freq, stored, classes):
+    sens = stored.shape[0]
+    per = sens // NW
     edge = jax.ShapeDtypeStruct((PX, 16, 128), BF16)
     edge_spec = pl.BlockSpec((PX, 16, 128), lambda i: (0, 0, 0))
     return pl.pallas_call(
         adjoint_body,
-        grid=(PX // 2,),
-        in_specs=[WHOLE] * 4,
-        out_specs=(WHOLE, WHOLE, edge_spec, edge_spec),
+        grid=(NW,),
+        in_specs=[SCALARS, WHOLE, WHOLE, pl.BlockSpec(memory_space=pltpu.HBM), WHOLE],
+        out_specs=(WHOLE, WHOLE, WHOLE, edge_spec, edge_spec),
         out_shape=(
+            jax.ShapeDtypeStruct((PX, sens * FREQ * 2, PY), BF16),
             jax.ShapeDtypeStruct((PX, COLS, PY), F32),
             jax.ShapeDtypeStruct((PX, 3, STRIP, 128), F32),
             edge,
             edge,
         ),
-        scratch_shapes=[pltpu.VMEM((COLS, NW * KW), BF16)],
-        compiler_params=params(30),
-    )(gathered, freq, ops, classes)
+        scratch_shapes=[
+            pltpu.VMEM((2, FREQ, per, 2, PX, PY), BF16),
+            pltpu.SemaphoreType.DMA((2,)),
+            pltpu.VMEM((COLS, KW), BF16),
+        ],
+        compiler_params=params(24),
+    )(inv, gathered, freq, stored, classes)
 
 
 XROWS = COLS + 16 + 3 * STRIP
@@ -148,7 +138,7 @@
         in_specs=[WHOLE] * 5,
         out_specs=(WHOLE, pl.BlockSpec(), pl.BlockSpec()),
         out_shape=(jax.ShapeDtypeStruct((PX, 3, STRIP, 128), F32), send, send),
-        compiler_params=params(30),
+        compiler_params=params(8),
     )(field, strips, before, after, classes)
 
 
@@ -247,17 +237,23 @@
             jax.ShapeDtypeStruct((COLS, PX, PY), BF16),
         ),
         scratch_shapes=[pltpu.VMEM((ext, 5, 8, PY), F32), pltpu.VMEM((ext, 5, STRIP, PY), F32)],
-        compiler_params=params(30),
+        compiler_params=params(12),
     )(table, field, strips, above, below, classes)
 
 
-def forward_body(prior, ops, out):
+def forward_body(prior, ops, keep, send):
     group = pl.program_id(0)
+    core = lax.axis_index("core")
     rows = pl.ds(pl.multiple_of(group * KW, KW), KW)
     left = jnp.concatenate([prior[x] for x in range(PX)], axis=1)
     right = jnp.concatenate([ops[x, rows, :] for x in range(PX)], axis=1)
     nt = (((1,), (1,)), ((), ()))
-    out[0] = lax.dot_general(left, right, nt, preferred_element_type=F32).astype(BF16)
+    total = lax.dot_general(left, right, nt, preferred_element_type=F32)
+    for chip in range(8):
+        even = total[chip * 32 : chip * 32 + 16]
+        odd = total[chip * 32 + 16 : chip * 32 + 32]
+        keep[group * 8 + chip] = jnp.where(core == 0, even, odd)
+        send[group * 8 + chip] = jnp.where(core == 0, odd, even).astype(BF16)
 
 
 def forward(prior, ops):
@@ -265,10 +261,20 @@
         forward_body,
         grid=(NW,),
         in_specs=[WHOLE, WHOLE],
-        out_specs=pl.BlockSpec((1, COLS, KW), lambda i: (i, 0, 0)),
-        out_shape=jax.ShapeDtypeStruct((NW, COLS, KW), BF16),
-        compiler_params=params(30),
+        out_specs=(WHOLE, WHOLE),
+        out_shape=(
+            jax.ShapeDtypeStruct((64, 16, KW), F32),
+            jax.ShapeDtypeStruct((64, 16, KW), BF16),
+        ),
+        compiler_params=params(16),
     )(prior, ops)
+
+
+def reduced(keep, send):
+    got = lax.ppermute(send, "core", [(0, 1), (1, 0)])
+    chip = (keep + got.astype(F32)).astype(BF16)
+    pieces = lax.all_to_all(chip, CHIPS, 0, 0, tiled=True)
+    return jnp.sum(pieces.astype(F32), axis=0)
 
 
 def shifted(value, axis, step):
@@ -279,8 +285,8 @@
 def on_device(seafloor_ops, sensor_data, column_freq, row_owner, coef_class, coef_table):
     sens = seafloor_ops.shape[0]
     per, own = sensor_data.shape[0], sensor_data.shape[3]
-    quad_weight = 2.0 * sens / (PX * lax.axis_size("wide") * PY * lax.axis_size("narrow"))
-    my_freq = lax.dynamic_slice_in_dim(column_freq, lax.axis_index("narrow") * own, own)
+    quad_weight = 2.0 * sens / (PX * lax.axis_size(WIDE) * PY * lax.axis_size(NARROW))
+    my_freq = lax.dynamic_slice_in_dim(column_freq, lax.axis_index(NARROW) * own, own)
     mask = my_freq[None, None, None, :] == jnp.arange(FREQ, dtype=jnp.int32)[None, :, None, None]
     chosen = jnp.sum(jnp.where(mask, sensor_data, 0).astype(F32), axis=1).astype(BF16)
     block = chosen.reshape(per * 2, own).T
@@ -291,34 +297,34 @@
     inverse = jnp.sum(jnp.where(row_owner[None, :] == ids[:, None], ids[None, :], 0), axis=1)
     classes = (coef_class + 1).astype(F32)
 
-    ops = relayout(seafloor_ops, inverse)
-    field, strips, y_up, y_down = adjoint(gathered, column_freq.reshape(COLS, 1), ops, classes)
-    before = shifted(y_up, "narrow", 1)
-    after = shifted(y_down, "narrow", -1)
+    ops, field, strips, y_up, y_down = adjoint(
+        inverse, gathered, column_freq.reshape(COLS, 1), seafloor_ops, classes
+    )
+    before = shifted(y_up, NARROW, 1)
+    after = shifted(y_down, NARROW, -1)
     strips, x_up, x_down = edges(field, strips, before, after, classes)
-    above = shifted(x_up, "wide", 1)
-    below = shifted(x_down, "wide", -1)
+    above = shifted(x_up, WIDE, 1)
+    below = shifted(x_down, WIDE, -1)
     prior, prior_field = sweeps(coef_table, field, strips, above, below, classes)
-    partial_value = forward(prior, ops)
-    pieces = lax.all_to_all(partial_value.reshape(128, own, KW), BOTH, 0, 0, tiled=True)
-    total = jnp.sum(pieces.astype(F32), axis=0) * quad_weight
+    total = reduced(*forward(prior, ops)) * quad_weight
     hessian = total.astype(BF16).reshape(own, FREQ, per, 2).transpose(2, 1, 3, 0)
     return hessian, prior_field
 
 
 def solution(mesh):
+    fine = jax.sharding.Mesh(mesh.devices.reshape(2, 4, 4, 2, 2), BOTH)
     placed = (
-        P(None, None, None, "wide", "narrow"),
-        P("wide", None, None, "narrow"),
+        P(None, None, None, WIDE, NARROW),
+        P(WIDE, None, None, NARROW),
         P(),
         P(),
-        P("wide", "narrow"),
+        P(WIDE, NARROW),
         P(),
     )
     return jax.shard_map(
         on_device,
-        mesh=mesh,
+        mesh=fine,
         in_specs=placed,
-        out_specs=(P("wide", None, None, "narrow"), P(None, "wide", "narrow")),
+        out_specs=(P(WIDE, None, None, NARROW), P(None, WIDE, NARROW)),
         check_vma=False,
     )

time: 138 us -> 115 us (0.83)
  the two profiles are of different devices: /device:TPU:1 before, /device:TPU:0 now
where the time goes in v2:
time: 115 us
  Pallas kernels  32.9 us (29%)
  blocking collectives  31.2 us (27%)
  waiting for transfers between devices  22.8 us (20%)
  starting transfers between devices  20.6 us (18%)
  local copies, waits for them, and re-layouts  3.47 us (3%)
  other arithmetic  3.04 us (3%)
    all_to_all x1, blocking collectives, reduced(): pieces = lax.all_to_all(chip, CHIPS, 0, 0, tiled=True)  31.2 us
    pallas_call x1, Pallas kernels, adjoint(): pl.pallas_call(adjoint_body, grid=(NW,), in_specs=[SCALARS, WHOLE, WHOLE,...  18.7 us
    all_to_all x1, starting transfers between devices, on_device(): lax.all_to_all(sent, BOTH, 0, 0, tiled=True).reshape(NW, COLS, per * 2)  11.2 us
    all_to_all x1, waiting for transfers between devices, on_device(): lax.all_to_all(sent, BOTH, 0, 0, tiled=True).reshape(NW, COLS, per * 2)  10.4 us
    ppermute x4, waiting for transfers between devices, shifted(): lax.ppermute(value, axis, [(i, i + step) for i in range(size) if 0 <= i +...  10.1 us
    pallas_call x1, Pallas kernels, sweeps(): pl.pallas_call(sweep_body, in_specs=[SCALARS] + [WHOLE] * 5, out_specs=(W...  8.05 us
    ppermute x4, starting transfers between devices, shifted(): lax.ppermute(value, axis, [(i, i + step) for i in range(size) if 0 <= i +...  6.33 us
    pallas_call x1, Pallas kernels, forward(): pl.pallas_call(forward_body, grid=(NW,), in_specs=[WHOLE, WHOLE], out_spe...  5.97 us
  transfers between devices with their start and end apart: 6, of which 5 were waited for; matrix products, arithmetic and copies ran while one was open for 2% of the time, Pallas kernels for 0%

profile of v2, /device:TPU:0, one launch (start us, length us, event | category | flops | bytes accessed | tf_op | source)
XLA Modules:
  0.0 114.7 jit_solution(12508750138409805732)
XLA Ops:
  0.6 0.8 dynamic_slice.3
  1.4 0.8 select_reduce_fusion.1
  2.2 0.1 copy.16
  2.3 0.1 copy.17
  2.4 0.9 broadcast_in_dim.39
  3.3 11.2 %all-to-all-start = ((bf16[128,16,128]{2,1,0:T(8,128)(2,1)}), bf16[128,16,128]{2,1,0:T(8,128)(2,1)S(1)}, u32[]{:S(2)}, u32[]{:S(2)}) async-start(bf16[128,16,128]{2,1,0:T(8,128)(2,1)} %broadcast_in_dim.39), calls=%async_computation | async-start | bytes 1048576 | tf_op jit(solution)/shard_map/all_to_all | solution.py:294
  14.5 0.8 copy.18.freq
  15.3 0.9 select_reduce_fusion.inv
  16.2 0.7 add_convert_fusion.1.classes
  16.9 10.4 %all-to-all-done = bf16[128,16,128]{2,1,0:T(8,128)(2,1)S(1)} async-done(((bf16[128,16,128]{2,1,0:T(8,128)(2,1)}), bf16[128,16,128]{2,1,0:T(8,128)(2,1)S(1)}, u32[]{:S(2)}, u32[]{:S(2)}) %all-to-all-start) | async-done | bytes 524320 | tf_op jit(solution)/shard_map/all_to_all | solution.py:294
  27.2 18.7 %shard_map.77 = (bf16[16,4096,128]{2,1,0:T(8,128)(2,1)S(1)}, f32[16,256,128]{2,1,0:T(8,128)S(1)}, f32[16,3,24,128]{3,2,1,0:T(8,128)S(1)}, bf16[16,16,128]{2,1,0:T(8,128)(2,1)S(1)}, bf16[16,16,128]{2,1,0:T(8,128)(2,1)S(1)}) custom-call(s32[512]{0:T(512)S(1)} %select_reduce_fusion.inv, bf16[8,256,128]{2,1,0:T(8,128)(2,1)S(1)} %bitcast.8, ...), custom_call_target="tpu_custom_call" | custom-call | tf_op jit(solution)/shard_map/pallas_call | solution.py:94
  45.9 0.0 copy-start
  45.9 2.0 %collective-permute-start = (bf16[16,16,128]{2,1,0:T(8,128)(2,1)S(1)}, bf16[16,16,128]{2,1,0:T(8,128)(2,1)S(1)}, u32[]{:S(2)}, u32[]{:S(2)}) collective-permute-start(bf16[16,16,128]{2,1,0:T(8,128)(2,1)S(1)} %get-tuple-element.16), channel_id=1, source_target_pairs={{0,1},{1,2},{2,3},{3,4},{4,5},{5,6},{6,7},{7,8},{8,9},{9,10},{10,1... | collective-permute-start | bytes 196616 | tf_op jit(solution)/shard_map/ppermute | solution.py:282
  48.0 1.3 %collective-permute-start.1 = (bf16[16,16,128]{2,1,0:T(8,128)(2,1)S(1)}, bf16[16,16,128]{2,1,0:T(8,128)(2,1)S(1)}, u32[]{:S(2)}, u32[]{:S(2)}) collective-permute-start(bf16[16,16,128]{2,1,0:T(8,128)(2,1)S(1)} %get-tuple-element.17), channel_id=1, source_target_pairs={{1,0},{2,1},{3,2},{4,3},{5,4},{6,5},{7,6},{8,7},{9,8},{10,9},{11,1... | collective-permute-start | bytes 196616 | tf_op jit(solution)/shard_map/ppermute | solution.py:282
  49.3 0.0 collective-permute-done.before
  49.3 3.2 %collective-permute-done.1.after = bf16[16,16,128]{2,1,0:T(8,128)(2,1)S(1)} collective-permute-done((bf16[16,16,128]{2,1,0:T(8,128)(2,1)S(1)}, bf16[16,16,128]{2,1,0:T(8,128)(2,1)S(1)}, u32[]{:S(2)}, u32[]{:S(2)}) %collective-permute-start.1) | collective-permute-done | bytes 65568 | tf_op jit(solution)/shard_map/ppermute | solution.py:282
  52.4 0.1 shard_map.78
  52.6 1.7 %collective-permute-start.2 = (bf16[3,344,128]{2,1,0:T(8,128)(2,1)S(1)}, bf16[3,344,128]{2,1,0:T(8,128)(2,1)S(1)}, u32[]{:S(2)}, u32[]{:S(2)}) collective-permute-start(bf16[3,344,128]{2,1,0:T(8,128)(2,1)S(1)} %get-tuple-element.19), channel_id=1, source_target_pairs={{0,16},{16,32},{32,48},{48,64},{64,80},{80,96},{96,112},{1,17},{17... | collective-permute-start | bytes 792584 | tf_op jit(solution)/shard_map/ppermute | solution.py:282
  54.3 1.3 %collective-permute-start.3 = (bf16[3,344,128]{2,1,0:T(8,128)(2,1)S(1)}, bf16[3,344,128]{2,1,0:T(8,128)(2,1)S(1)}, u32[]{:S(2)}, u32[]{:S(2)}) collective-permute-start(bf16[3,344,128]{2,1,0:T(8,128)(2,1)S(1)} %get-tuple-element.20), channel_id=1, source_target_pairs={{16,0},{32,16},{48,32},{64,48},{80,64},{96,80},{112,96},{17,1},{33... | collective-permute-start | bytes 792584 | tf_op jit(solution)/shard_map/ppermute | solution.py:282
  55.6 2.6 %collective-permute-done.2.above = bf16[3,344,128]{2,1,0:T(8,128)(2,1)S(1)} collective-permute-done((bf16[3,344,128]{2,1,0:T(8,128)(2,1)S(1)}, bf16[3,344,128]{2,1,0:T(8,128)(2,1)S(1)}, u32[]{:S(2)}, u32[]{:S(2)}) %collective-permute-start.2) | collective-permute-done | bytes 264224 | tf_op jit(solution)/shard_map/ppermute | solution.py:282
  58.2 4.4 %collective-permute-done.3.below = bf16[3,344,128]{2,1,0:T(8,128)(2,1)S(1)} collective-permute-done((bf16[3,344,128]{2,1,0:T(8,128)(2,1)S(1)}, bf16[3,344,128]{2,1,0:T(8,128)(2,1)S(1)}, u32[]{:S(2)}, u32[]{:S(2)}) %collective-permute-start.3) | collective-permute-done | bytes 264224 | tf_op jit(solution)/shard_map/ppermute | solution.py:282
  62.6 0.0 copy-done
  62.6 8.1 %shard_map.79 = (bf16[16,256,128]{2,1,0:T(8,128)(2,1)S(1)}, bf16[256,16,128]{2,1,0:T(8,128)(2,1)}) custom-call(f32[8]{0:T(128)S(1)} %copy-done, f32[16,256,128]{2,1,0:T(8,128)S(1)} %get-tuple-element.14.field, f32[16,3,24,128]{3,2,1,0:T(8,128)S(1)} %get-tuple-element.18.strips, bf16[3,344,128]{2,1,0:T(8,128)(2,1)S(1)} %collective-permute-done.2.above, ...), custom_call_target="tpu_custom_call" | custom-call | tf_op jit(solution)/shard_map/pallas_call | solution.py:231
  70.7 6.0 %shard_map.80 = (f32[64,16,512]{2,1,0:T(8,128)S(1)}, bf16[64,16,512]{2,1,0:T(8,128)(2,1)S(1)}) custom-call(bf16[16,256,128]{2,1,0:T(8,128)(2,1)S(1)} %get-tuple-element.21.prior, bf16[16,4096,128]{2,1,0:T(8,128)(2,1)S(1)} %get-tuple-element.22.ops), custom_call_target="tpu_custom_call" | custom-call | tf_op jit(solution)/shard_map/pallas_call | solution.py:260
  76.6 3.1 %collective-permute-start.4 = (bf16[64,16,512]{2,1,0:T(8,128)(2,1)S(1)}, bf16[64,16,512]{2,1,0:T(8,128)(2,1)S(1)}, u32[]{:S(2)}, u32[]{:S(2)}) collective-permute-start(bf16[64,16,512]{2,1,0:T(8,128)(2,1)S(1)} %get-tuple-element.24), channel_id=1, source_target_pairs={{0,1},{1,0},{2,3},{3,2},{4,5},{5,4},{6,7},{7,6},{8,9},{9,8},{10,11... | collective-permute-start | bytes 3145736 | tf_op jit(solution)/shard_map/ppermute | solution.py:274
  79.7 2.3 %collective-permute-done.4 = bf16[64,16,512]{2,1,0:T(8,128)(2,1)S(1)} collective-permute-done((bf16[64,16,512]{2,1,0:T(8,128)(2,1)S(1)}, bf16[64,16,512]{2,1,0:T(8,128)(2,1)S(1)}, u32[]{:S(2)}, u32[]{:S(2)}) %collective-permute-start.4) | collective-permute-done | bytes 1048608 | tf_op jit(solution)/shard_map/ppermute | solution.py:274
  82.0 0.4 add_convert_fusion
  82.5 31.2 %all_to_all.10 = bf16[64,16,512]{2,1,0:T(8,128)(2,1)S(1)} all-to-all(bf16[64,16,512]{2,1,0:T(8,128)(2,1)S(1)} %add_convert_fusion), channel_id=1, replica_groups=mesh['z_lo'=2,'x'=4,'y'=4,'z_hi'=2,'core'=2] {'z_lo','x','y','z_hi'}, dimensions={0} | all-to-all | bytes 2097152 | tf_op jit(solution)/shard_map/all_to_all | solution.py:276
  113.7 0.2 convert_reduce_fusion
  113.8 0.1 copy.19
  114.0 0.7 copy.20
  (2 shorter events, 0.0 us)
Async XLA Ops:
  3.3 23.9 %all-to-all-start = ((bf16[128,16,128]{2,1,0:T(8,128)(2,1)}), bf16[128,16,128]{2,1,0:T(8,128)(2,1)S(1)}, u32[]{:S(2)}, u32[]{:S(2)}) async-start(bf16[128,16,128]{2,1,0:T(8,128)(2,1)} %broadcast_in_dim.39), calls=%async_computation | async-start | bytes 1048576 | tf_op jit(solution)/shard_map/all_to_all | solution.py:294
  45.9 16.7 %copy-start = (f32[8]{0:T(128)S(1)}, f32[8]{0:T(128)}, u32[]{:S(2)}) copy-start(f32[8]{0:T(128)} %table.1) | copy-start | bytes 100
  45.9 3.3 %collective-permute-start = (bf16[16,16,128]{2,1,0:T(8,128)(2,1)S(1)}, bf16[16,16,128]{2,1,0:T(8,128)(2,1)S(1)}, u32[]{:S(2)}, u32[]{:S(2)}) collective-permute-start(bf16[16,16,128]{2,1,0:T(8,128)(2,1)S(1)} %get-tuple-element.16), channel_id=1, source_target_pairs={{0,1},{1,2},{2,3},{3,4},{4,5},{5,6},{6,7},{7,8},{8,9},{9,10},{10,1... | collective-permute-start | bytes 196616 | tf_op jit(solution)/shard_map/ppermute | solution.py:282
  48.0 4.5 %collective-permute-start.1 = (bf16[16,16,128]{2,1,0:T(8,128)(2,1)S(1)}, bf16[16,16,128]{2,1,0:T(8,128)(2,1)S(1)}, u32[]{:S(2)}, u32[]{:S(2)}) collective-permute-start(bf16[16,16,128]{2,1,0:T(8,128)(2,1)S(1)} %get-tuple-element.17), channel_id=1, source_target_pairs={{1,0},{2,1},{3,2},{4,3},{5,4},{6,5},{7,6},{8,7},{9,8},{10,9},{11,1... | collective-permute-start | bytes 196616 | tf_op jit(solution)/shard_map/ppermute | solution.py:282
  52.6 5.6 %collective-permute-start.2 = (bf16[3,344,128]{2,1,0:T(8,128)(2,1)S(1)}, bf16[3,344,128]{2,1,0:T(8,128)(2,1)S(1)}, u32[]{:S(2)}, u32[]{:S(2)}) collective-permute-start(bf16[3,344,128]{2,1,0:T(8,128)(2,1)S(1)} %get-tuple-element.19), channel_id=1, source_target_pairs={{0,16},{16,32},{32,48},{48,64},{64,80},{80,96},{96,112},{1,17},{17... | collective-permute-start | bytes 792584 | tf_op jit(solution)/shard_map/ppermute | solution.py:282
  54.3 8.3 %collective-permute-start.3 = (bf16[3,344,128]{2,1,0:T(8,128)(2,1)S(1)}, bf16[3,344,128]{2,1,0:T(8,128)(2,1)S(1)}, u32[]{:S(2)}, u32[]{:S(2)}) collective-permute-start(bf16[3,344,128]{2,1,0:T(8,128)(2,1)S(1)} %get-tuple-element.20), channel_id=1, source_target_pairs={{16,0},{32,16},{48,32},{64,48},{80,64},{96,80},{112,96},{17,1},{33... | collective-permute-start | bytes 792584 | tf_op jit(solution)/shard_map/ppermute | solution.py:282
  76.6 5.4 %collective-permute-start.4 = (bf16[64,16,512]{2,1,0:T(8,128)(2,1)S(1)}, bf16[64,16,512]{2,1,0:T(8,128)(2,1)S(1)}, u32[]{:S(2)}, u32[]{:S(2)}) collective-permute-start(bf16[64,16,512]{2,1,0:T(8,128)(2,1)S(1)} %get-tuple-element.24), channel_id=1, source_target_pairs={{0,1},{1,0},{2,3},{3,2},{4,5},{5,4},{6,7},{7,6},{8,9},{9,8},{10,11... | collective-permute-start | bytes 3145736 | tf_op jit(solution)/shard_map/ppermute | solution.py:274

commit v3 on v2

v3 whole, which is shorter than its diff:
```python
import jax
import jax.numpy as jnp
from jax import lax
from jax.experimental import pallas as pl
from jax.experimental.pallas import tpu as pltpu
from jax.sharding import PartitionSpec as P

SWEEPS = 3
WIDE, NARROW = ("z_lo", "x"), ("y", "z_hi", "core")
BOTH = WIDE + NARROW
CHIPS = WIDE + NARROW[:2]
F32 = jnp.float32
BF16 = jnp.bfloat16
WHOLE = pl.BlockSpec(memory_space=pltpu.VMEM)
SCALARS = pl.BlockSpec(memory_space=pltpu.SMEM)
PX, PY = 16, 128
COLS, FREQ, NW, KW = 256, 4, 8, 512
STRIP = 24


def params(mib):
    return pltpu.CompilerParams(vmem_limit_bytes=mib << 20)


def strip_lane(rows):
    left = (rows >= 3) & (rows < 12)
    right = (rows >= 12) & (rows < 21)
    return jnp.where(left, rows - 3, jnp.where(right, rows + (PY - 21), -1))


def adjoint_body(inv, gathered, freq, stored, classes, ops, field, strips, y_a, y_b, x_a, x_b, buf, sems, probes):
    group = pl.program_id(0)
    per = buf.shape[2]

    def fetch(which, slot):
        def one(j, _):
            sensor = inv[which * per + j]
            pltpu.make_async_copy(stored.at[sensor], buf.at[slot, :, j], sems.at[slot]).start()
            return 0

        lax.fori_loop(0, per, one, 0, unroll=8)

    @pl.when(group == 0)
    def _():
        fetch(0, 0)
        field[...] = jnp.zeros_like(field)

    @pl.when(group + 1 < pl.num_programs(0))
    def _():
        fetch(group + 1, (group + 1) % 2)

    slot = group % 2
    block = gathered[group]
    for f in range(FREQ):
        probes[:, f * 128 : f * 128 + 128] = jnp.where(freq[...] == f, block, 0).astype(BF16)
    pltpu.make_async_copy(buf.at[slot], buf.at[slot], sems.at[slot]).wait()
    for f in range(0, FREQ, 2):
        laid = jnp.swapaxes(buf[slot, f : f + 2].reshape(per * 4, PX, PY), 0, 1)
        start = pl.multiple_of(group * KW + f * per * 2, per * 4)
        ops[:, pl.ds(start, per * 4), :] = laid
        for x in range(0, PX, 2):
            pair = jnp.concatenate([laid[x], laid[x + 1]], axis=1)
            both = jnp.dot(probes[:, f * 128 : f * 128 + 256], pair, preferred_element_type=F32)
            field[x] += both[:, :PY]
            field[x + 1] += both[:, PY:]

    @pl.when(group == pl.num_programs(0) - 1)
    def _():
        line = lax.broadcasted_iota(jnp.int32, (STRIP, 2 * PY), 0)
        lanes = lax.broadcasted_iota(jnp.int32, (STRIP, 2 * PY), 1)
        pick = (strip_lane(line) == lanes % PY).astype(F32).astype(BF16)
        nt = (((1,), (1,)), ((), ()))
        for x in range(PX):
            mine = field[x]
            high = mine.astype(BF16)
            low = (mine - high.astype(F32)).astype(BF16)
            strip = lax.dot_general(pick, jnp.concatenate([high, low], axis=1), nt, preferred_element_type=F32)
            row = jnp.broadcast_to(classes[x : x + 1, :], (PY, PY)).astype(BF16)
            label = lax.dot_general(pick[:, :PY], row, nt, preferred_element_type=F32)
            parts = (strip[:, :128], strip[:, 128:], label)
            for t in range(3):
                strips[x, t] = parts[t]
            pad = jnp.zeros((7, 128), F32)
            up = jnp.concatenate([p[18:21] for p in parts] + [pad], axis=0).astype(BF16)
            down = jnp.concatenate([p[3:6] for p in parts] + [pad], axis=0).astype(BF16)
            even = lax.axis_index(NARROW[-1]) == 0
            y_a[x] = jnp.where(even, up, down)
            y_b[x] = jnp.where(even, down, up)
        even = lax.axis_index(WIDE[-1]) % 2 == 0
        for first, out in ((jnp.where(even, PX - 3, 0), x_a), (jnp.where(even, 0, PX - 3), x_b)):
            for j in range(3):
                out[j, :COLS] = field[first + j].astype(BF16)
                row = classes[pl.ds(first + j, 1), :]
                out[j, COLS : COLS + 16] = jnp.broadcast_to(row, (16, PY)).astype(BF16)


def adjoint(inv, gathered, freq, stored, classes):
    sens = stored.shape[0]
    per = sens // NW
    y_edge = jax.ShapeDtypeStruct((PX, 16, 128), BF16)
    x_edge = jax.ShapeDtypeStruct((3, COLS + 16, PY), BF16)
    return pl.pallas_call(
        adjoint_body,
        grid=(NW,),
        in_specs=[SCALARS, WHOLE, WHOLE, pl.BlockSpec(memory_space=pltpu.HBM), WHOLE],
        out_specs=(WHOLE,) * 7,
        out_shape=(
            jax.ShapeDtypeStruct((PX, sens * FREQ * 2, PY), BF16),
            jax.ShapeDtypeStruct((PX, COLS, PY), F32),
            jax.ShapeDtypeStruct((PX, 3, STRIP, 128), F32),
            y_edge,
            y_edge,
            x_edge,
            x_edge,
        ),
        scratch_shapes=[
            pltpu.VMEM((2, FREQ, per, 2, PX, PY), BF16),
            pltpu.SemaphoreType.DMA((2,)),
            pltpu.VMEM((COLS, KW), BF16),
        ],
        compiler_params=params(24),
    )(inv, gathered, freq, stored, classes)


SROWS = 80


def halves(even, first, second):
    return jnp.where(even, second, first), jnp.where(even, first, second)


def edges_body(strips, y_a, y_b, whole, s_a, s_b):
    even = lax.axis_index(NARROW[-1]) == 0
    for x in range(PX):
        low, high = halves(even, y_a[x].astype(F32), y_b[x].astype(F32))
        for t in range(3):
            at = slice(3 * t, 3 * t + 3)
            whole[x, t] = jnp.concatenate([low[at], strips[x, t, 3:21, :], high[at]], axis=0)
    even = lax.axis_index(WIDE[-1]) % 2 == 0
    pad = jnp.zeros((SROWS - 3 * STRIP, 128), F32)
    for first, out in ((jnp.where(even, PX - 3, 0), s_a), (jnp.where(even, 0, PX - 3), s_b)):
        for j in range(3):
            out[j] = jnp.concatenate([whole[first + j, t] for t in range(3)] + [pad], axis=0).astype(BF16)


def edges(strips, y_a, y_b):
    send = jax.ShapeDtypeStruct((3, SROWS, 128), BF16)
    return pl.pallas_call(
        edges_body,
        in_specs=[WHOLE] * 3,
        out_specs=(WHOLE,) * 3,
        out_shape=(jax.ShapeDtypeStruct((PX, 3, STRIP, 128), F32), send, send),
        compiler_params=params(8),
    )(strips, y_a, y_b)


def table_of(labels, table):
    kappa = jnp.zeros(labels.shape, F32)
    for j in range(8):
        kappa = jnp.where(labels == float(j + 1), table[j], kappa)
    return kappa


def weights(here, up, down, left, right):
    four = [jnp.minimum(here, n) for n in (up, down, left, right)]
    return [1.0 - (four[0] + four[1] + four[2] + four[3])] + four


def smooth(value, load, axis, size):
    for turn in range(SWEEPS):
        fresh = []
        for i in range(1, len(value) - 1):
            m = load(i + turn)
            mid = value[i]
            left = pltpu.roll(mid, 1, axis)
            right = pltpu.roll(mid, size - 1, axis)
            a = m[0] * mid + m[1] * value[i - 1]
            b = m[2] * value[i + 1] + m[3] * left
            fresh.append(a + (b + m[4] * right))
        value = fresh
    return value


def coefficients(kappa, axis, size, out):
    for i in range(1, PX + 5):
        k = kappa[i]
        ws = weights(k, kappa[i - 1], kappa[i + 1], pltpu.roll(k, 1, axis), pltpu.roll(k, size - 1, axis))
        for d in range(5):
            out[i, d] = ws[d]


def inner_body(table, field, x_a, x_b, classes, inner, coef):
    even = lax.axis_index(WIDE[-1]) % 2 == 0

    def halo(j, rows):
        return halves(even, x_a[j, rows, :].astype(F32), x_b[j, rows, :].astype(F32))

    label = [halo(j, slice(COLS, COLS + 8)) for j in range(3)]
    own = [jnp.broadcast_to(classes[x : x + 1, :], (8, PY)) for x in range(PX)]
    label = [v[0] for v in label] + own + [v[1] for v in label]
    coefficients([table_of(v, table) for v in label], 1, PY, coef)

    def columns(g, _):
        rows = pl.ds(pl.multiple_of(g * 16, 16), 16)
        ends = [halo(j, rows) for j in range(3)]
        value = [v[0] for v in ends] + [field[x, rows, :] for x in range(PX)] + [v[1] for v in ends]

        def load(i):
            return [jnp.concatenate([coef[i, d]] * 2, axis=0) for d in range(5)]

        value = smooth(value, load, 1, PY)
        for x in range(PX):
            inner[x, rows, :] = value[x].astype(BF16)
        return 0

    lax.fori_loop(0, COLS // 16, columns, 0)


def inner_sweeps(table, field, x_a, x_b, classes):
    return pl.pallas_call(
        inner_body,
        in_specs=[SCALARS] + [WHOLE] * 4,
        out_specs=WHOLE,
        out_shape=jax.ShapeDtypeStruct((PX, COLS, PY), BF16),
        scratch_shapes=[pltpu.VMEM((PX + 6, 5, 8, PY), F32)],
        compiler_params=params(12),
    )(table, field, x_a, x_b, classes)


def outer_body(table, whole, s_a, s_b, inner, prior, prior_out, coef):
    even = lax.axis_index(WIDE[-1]) % 2 == 0

    def strip_rows(t):
        rows = slice(t * STRIP, (t + 1) * STRIP)
        ends = [halves(even, s_a[j, rows, :].astype(F32), s_b[j, rows, :].astype(F32)) for j in range(3)]
        return [v[0] for v in ends] + [whole[x, t] for x in range(PX)] + [v[1] for v in ends]

    coefficients([table_of(v, table) for v in strip_rows(2)], 0, STRIP, coef)
    edge = [smooth(strip_rows(t), lambda i: [coef[i, d] for d in range(5)], 0, STRIP) for t in range(2)]
    rows = lax.broadcasted_iota(jnp.int32, (STRIP, PY), 0)
    lanes = lax.broadcasted_iota(jnp.int32, (STRIP, PY), 1)
    pick = (strip_lane(rows) == lanes).astype(F32).astype(BF16)
    lane = lax.broadcasted_iota(jnp.int32, (COLS, PY), 1)
    middle = (lane >= 3) & (lane < PY - 3)
    tn = (((0,), (0,)), ((), ()))
    for x in range(PX):
        both = jnp.concatenate([edge[0][x], edge[1][x]], axis=1).astype(BF16)
        at_edge = lax.dot_general(both, pick, tn, preferred_element_type=F32)
        prior[x] = jnp.where(middle, inner[x].astype(F32), at_edge).astype(BF16)
    prior_out[...] = jnp.swapaxes(prior[...], 0, 1)


def outer_sweeps(table, whole, s_a, s_b, inner):
    return pl.pallas_call(
        outer_body,
        in_specs=[SCALARS] + [WHOLE] * 4,
        out_specs=(WHOLE, pl.BlockSpec()),
        out_shape=(
            jax.ShapeDtypeStruct((PX, COLS, PY), BF16),
            jax.ShapeDtypeStruct((COLS, PX, PY), BF16),
        ),
        scratch_shapes=[pltpu.VMEM((PX + 6, 5, STRIP, PY), F32)],
        compiler_params=params(12),
    )(table, whole, s_a, s_b, inner)


def forward_body(prior, ops, keep, send):
    group = pl.program_id(0)
    core = lax.axis_index("core")
    rows = pl.ds(pl.multiple_of(group * KW, KW), KW)
    left = jnp.concatenate([prior[x] for x in range(PX)], axis=1)
    right = jnp.concatenate([ops[x, rows, :] for x in range(PX)], axis=1)
    nt = (((1,), (1,)), ((), ()))
    total = lax.dot_general(left, right, nt, preferred_element_type=F32)
    for chip in range(8):
        even = total[chip * 32 : chip * 32 + 16]
        odd = total[chip * 32 + 16 : chip * 32 + 32]
        keep[group * 8 + chip] = jnp.where(core == 0, even, odd)
        send[group * 8 + chip] = jnp.where(core == 0, odd, even).astype(BF16)


def forward(prior, ops):
    return pl.pallas_call(
        forward_body,
        grid=(NW,),
        in_specs=[WHOLE, WHOLE],
        out_specs=(WHOLE, WHOLE),
        out_shape=(
            jax.ShapeDtypeStruct((64, 16, KW), F32),
            jax.ShapeDtypeStruct((64, 16, KW), BF16),
        ),
        compiler_params=params(16),
    )(prior, ops)


def reduced(keep, send):
    got = lax.ppermute(send, "core", [(0, 1), (1, 0)])
    chip = (keep + got.astype(F32)).astype(BF16)
    pieces = lax.all_to_all(chip, CHIPS, 0, 0, tiled=True)
    return jnp.sum(pieces.astype(F32), axis=0)


def swapped(first, second, axis):
    size = lax.axis_size(axis)
    odd = [(i, i + 1) for i in range(1, size - 1, 2)]
    got = lax.ppermute(first, axis, [(i, i ^ 1) for i in range(size)])
    return got, lax.ppermute(second, axis, odd + [(j, i) for i, j in odd])


def on_device(seafloor_ops, sensor_data, column_freq, row_owner, coef_class, coef_table):
    sens = seafloor_ops.shape[0]
    per, own = sensor_data.shape[0], sensor_data.shape[3]
    quad_weight = 2.0 * sens / (PX * lax.axis_size(WIDE) * PY * lax.axis_size(NARROW))
    my_freq = lax.dynamic_slice_in_dim(column_freq, lax.axis_index(NARROW) * own, own)
    mask = my_freq[None, None, None, :] == jnp.arange(FREQ, dtype=jnp.int32)[None, :, None, None]
    chosen = jnp.sum(jnp.where(mask, sensor_data, 0).astype(F32), axis=1).astype(BF16)
    block = chosen.reshape(per * 2, own).T
    sent = jnp.broadcast_to(block[None], (128,) + block.shape)
    gathered = lax.all_to_all(sent, BOTH, 0, 0, tiled=True).reshape(NW, COLS, per * 2)

    ids = jnp.arange(sens, dtype=jnp.int32)
    inverse = jnp.sum(jnp.where(row_owner[None, :] == ids[:, None], ids[None, :], 0), axis=1)
    classes = (coef_class + 1).astype(F32)

    ops, field, strips, y_a, y_b, x_a, x_b = adjoint(
        inverse, gathered, column_freq.reshape(COLS, 1), seafloor_ops, classes
    )
    y_a, y_b = swapped(y_a, y_b, NARROW)
    x_a, x_b = swapped(x_a, x_b, WIDE)
    whole, s_a, s_b = edges(strips, y_a, y_b)
    s_a, s_b = swapped(s_a, s_b, WIDE)
    inner = inner_sweeps(coef_table, field, x_a, x_b, classes)
    prior, prior_field = outer_sweeps(coef_table, whole, s_a, s_b, inner)
    total = reduced(*forward(prior, ops)) * quad_weight
    hessian = total.astype(BF16).reshape(own, FREQ, per, 2).transpose(2, 1, 3, 0)
    return hessian, prior_field


def solution(mesh):
    fine = jax.sharding.Mesh(mesh.devices.reshape(2, 4, 4, 2, 2), BOTH)
    placed = (
        P(None, None, None, WIDE, NARROW),
        P(WIDE, None, None, NARROW),
        P(),
        P(),
        P(WIDE, NARROW),
        P(),
    )
    return jax.shard_map(
        on_device,
        mesh=fine,
        in_specs=placed,
        out_specs=(P(WIDE, None, None, NARROW), P(None, WIDE, NARROW)),
        check_vma=False,
    )
```

time: 115 us -> 104 us (0.904)
  waiting for transfers between devices: 22.8 us -> 13.4 us
  Pallas kernels: 32.9 us -> 29.5 us
  starting transfers between devices: 20.6 us -> 23.9 us
  blocking collectives: 31.2 us -> 29.9 us
    ppermute x4 -> x6, waiting for transfers between devices: 10.1 us -> 0.73 us  [the longest x3 0.72 us: swapped(): got = lax.ppermute(first, axis, [(i, i ^ 1) for i in range(size)])]
    pallas_call x1, Pallas kernels: 18.7 us -> 14.7 us  [adjoint(): pl.pallas_call(adjoint_body, grid=(NW,), in_specs=[SCALARS, WHOLE, WHOLE,...]
    ppermute x1, starting transfers between devices: 3.09 us -> 6.37 us  [reduced(): got = lax.ppermute(send, 'core', [(0, 1), (1, 0)])]
    all_to_all x1, blocking collectives: 31.2 us -> 29.9 us  [reduced(): pieces = lax.all_to_all(chip, CHIPS, 0, 0, tiled=True)]
    pallas_call x2 -> x3, Pallas kernels: 8.19 us -> 8.76 us  [the longest x1 5.73 us: inner_sweeps(): pl.pallas_call(inner_body, in_specs=[SCALARS] + [WHOLE] * 4, out_specs=WH...]
    ppermute x4 -> x6, starting transfers between devices: 6.33 us -> 6.4 us  [the longest x3 4.42 us: swapped(): got = lax.ppermute(first, axis, [(i, i ^ 1) for i in range(size)])]
  transfers between devices with their start and end apart: 6 -> 8, of which waited for: 5 -> 4; matrix products, arithmetic and copies ran while one was open for 2% -> 2% of each run, Pallas kernels for 0% -> 6%
where the time goes in v3:
time: 104 us
  blocking collectives  29.9 us (29%)
  Pallas kernels  29.5 us (28%)
  starting transfers between devices  23.9 us (23%)
  waiting for transfers between devices  13.4 us (13%)
  local copies, waits for them, and re-layouts  3.47 us (3%)
  other arithmetic  2.99 us (3%)
    all_to_all x1, blocking collectives, reduced(): pieces = lax.all_to_all(chip, CHIPS, 0, 0, tiled=True)  29.9 us
    pallas_call x1, Pallas kernels, adjoint(): pl.pallas_call(adjoint_body, grid=(NW,), in_specs=[SCALARS, WHOLE, WHOLE,...  14.7 us
    all_to_all x1, starting transfers between devices, on_device(): lax.all_to_all(sent, BOTH, 0, 0, tiled=True).reshape(NW, COLS, per * 2)  11.2 us
    all_to_all x1, waiting for transfers between devices, on_device(): lax.all_to_all(sent, BOTH, 0, 0, tiled=True).reshape(NW, COLS, per * 2)  10.4 us
    ppermute x1, starting transfers between devices, reduced(): got = lax.ppermute(send, 'core', [(0, 1), (1, 0)])  6.37 us
    pallas_call x1, Pallas kernels, forward(): pl.pallas_call(forward_body, grid=(NW,), in_specs=[WHOLE, WHOLE], out_spe...  6.03 us
    pallas_call x1, Pallas kernels, inner_sweeps(): pl.pallas_call(inner_body, in_specs=[SCALARS] + [WHOLE] * 4, out_specs=WH...  5.73 us
    ppermute x3, starting transfers between devices, swapped(): got = lax.ppermute(first, axis, [(i, i ^ 1) for i in range(size)])  4.42 us
  transfers between devices with their start and end apart: 8, of which 4 were waited for; matrix products, arithmetic and copies ran while one was open for 2% of the time, Pallas kernels for 6%

profile of v3, /device:TPU:0, one launch (start us, length us, event | category | flops | bytes accessed | tf_op | source)
XLA Modules:
  0.0 103.9 jit_solution(11202956360202068934)
XLA Ops:
  0.6 0.8 dynamic_slice.3
  1.4 0.8 select_reduce_fusion.1
  2.2 0.1 copy.16
  2.3 0.1 copy.17
  2.4 0.9 broadcast_in_dim.39
  3.3 11.2 %all-to-all-start = ((bf16[128,16,128]{2,1,0:T(8,128)(2,1)}), bf16[128,16,128]{2,1,0:T(8,128)(2,1)S(1)}, u32[]{:S(2)}, u32[]{:S(2)}) async-start(bf16[128,16,128]{2,1,0:T(8,128)(2,1)} %broadcast_in_dim.39), calls=%async_computation | async-start | bytes 1048576 | tf_op jit(solution)/shard_map/all_to_all | solution.py:319
  14.5 0.8 copy.18.freq
  15.3 0.9 select_reduce_fusion.inv
  16.2 0.7 add_convert_fusion.1.classes
  16.9 10.4 %all-to-all-done = bf16[128,16,128]{2,1,0:T(8,128)(2,1)S(1)} async-done(((bf16[128,16,128]{2,1,0:T(8,128)(2,1)}), bf16[128,16,128]{2,1,0:T(8,128)(2,1)S(1)}, u32[]{:S(2)}, u32[]{:S(2)}) %all-to-all-start) | async-done | bytes 524320 | tf_op jit(solution)/shard_map/all_to_all | solution.py:319
  27.2 0.0 copy-start
  27.2 14.7 %shard_map.77 = (bf16[16,4096,128]{2,1,0:T(8,128)(2,1)S(1)}, f32[16,256,128]{2,1,0:T(8,128)S(1)}, f32[16,3,24,128]{3,2,1,0:T(8,128)S(1)}, bf16[16,16,128]{2,1,0:...) custom-call(s32[512]{0:T(512)S(1)} %select_reduce_fusion.inv, ...), custom_call_target="tpu_custom_call" | custom-call | tf_op jit(solution)/shard_map/pallas_call | solution.py:102
  41.9 0.1 collective-permute-start.4
  42.0 0.7 collective-permute-start.5
  42.7 0.2 collective-permute-start
  42.9 0.7 collective-permute-start.1
  43.6 0.5 collective-permute-done.y_a
  44.1 0.0 collective-permute-done.1.y_b
  44.1 0.1 shard_map.78
  44.2 4.1 %collective-permute-start.2 = (bf16[3,80,128]{2,1,0:T(8,128)(2,1)S(1)}, bf16[3,80,128]{2,1,0:T(8,128)(2,1)S(1)}, u32[]{:S(2)}, u32[]{:S(2)}) collective-permute-start(bf16[3,80,128]{2,1,0:T(8,128)(2,1)S(1)} %get-tuple-element.20), channel_id=1, source_target_pairs={{0,16},{16,0},{32,48},{48,32},{64,80},{80,64},{96,112},{112,96},{1... | collective-permute-start | bytes 184328 | tf_op jit(solution)/shard_map/ppermute | solution.py:306
  48.3 0.7 collective-permute-start.3
  49.0 0.2 collective-permute-done.4.x_a
  49.2 0.0 collective-permute-done.5.x_b
  49.2 0.0 copy-done
  49.2 5.7 %shard_map.79.inner = bf16[16,256,128]{2,1,0:T(8,128)(2,1)S(1)} custom-call(f32[8]{0:T(128)S(1)} %copy-done, f32[16,256,128]{2,1,0:T(8,128)S(1)} %get-tuple-element.22.field, bf16[3,272,128]{2,1,0:T(8,128)(2,1)S(1)} %collective-permute-done.4.x_a, bf16[3,272,128]{2,1,0:T(8,128)(2,1)S(1)} %collective-permute-done.5.x_b, f32[16,128]{1,0:T(8,128)S(1)} %add_convert_fusion.1.classes), custom_call_target="tpu_custom_call" | custom-call | tf_op jit(solution)/shard_map/pallas_call | solution.py:220
  54.9 0.0 collective-permute-done.2.s_a
  55.0 0.0 collective-permute-done.3.s_b
  55.0 2.9 %shard_map.80 = (bf16[16,256,128]{2,1,0:T(8,128)(2,1)S(1)}, bf16[256,16,128]{2,1,0:T(8,128)(2,1)}) custom-call(f32[8]{0:T(128)S(1)} %copy-done, f32[16,3,24,128]{3,2,1,0:T(8,128)S(1)} %get-tuple-element.19.whole, bf16[3,80,128]{2,1,0:T(8,128)(2,1)S(1)} %collective-permute-done.2.s_a, bf16[3,80,128]{2,1,0:T(8,128)(2,1)S(1)} %collective-permute-done.3.s_b, ...), custom_call_target="tpu_custom_call" | custom-call | tf_op jit(solution)/shard_map/pallas_call | solution.py:254
  57.9 6.0 %shard_map.81 = (f32[64,16,512]{2,1,0:T(8,128)S(1)}, bf16[64,16,512]{2,1,0:T(8,128)(2,1)S(1)}) custom-call(bf16[16,256,128]{2,1,0:T(8,128)(2,1)S(1)} %get-tuple-element.25.prior, bf16[16,4096,128]{2,1,0:T(8,128)(2,1)S(1)} %get-tuple-element.26.ops), custom_call_target="tpu_custom_call" | custom-call | tf_op jit(solution)/shard_map/pallas_call | solution.py:283
  63.9 6.4 %collective-permute-start.6 = (bf16[64,16,512]{2,1,0:T(8,128)(2,1)S(1)}, bf16[64,16,512]{2,1,0:T(8,128)(2,1)S(1)}, u32[]{:S(2)}, u32[]{:S(2)}) collective-permute-start(bf16[64,16,512]{2,1,0:T(8,128)(2,1)S(1)} %get-tuple-element.28), channel_id=1, source_target_pairs={{0,1},{1,0},{2,3},{3,2},{4,5},{5,4},{6,7},{7,6},{8,9},{9,8},{10,11... | collective-permute-start | bytes 3145736 | tf_op jit(solution)/shard_map/ppermute | solution.py:297
  70.3 2.3 %collective-permute-done.6 = bf16[64,16,512]{2,1,0:T(8,128)(2,1)S(1)} collective-permute-done((bf16[64,16,512]{2,1,0:T(8,128)(2,1)S(1)}, bf16[64,16,512]{2,1,0:T(8,128)(2,1)S(1)}, u32[]{:S(2)}, u32[]{:S(2)}) %collective-permute-start.6) | collective-permute-done | bytes 1048608 | tf_op jit(solution)/shard_map/ppermute | solution.py:297
  72.6 0.4 add_convert_fusion
  73.0 29.9 %all_to_all.10 = bf16[64,16,512]{2,1,0:T(8,128)(2,1)S(1)} all-to-all(bf16[64,16,512]{2,1,0:T(8,128)(2,1)S(1)} %add_convert_fusion), channel_id=1, replica_groups=mesh['z_lo'=2,'x'=4,'y'=4,'z_hi'=2,'core'=2] {'z_lo','x','y','z_hi'}, dimensions={0} | all-to-all | bytes 2097152 | tf_op jit(solution)/shard_map/all_to_all | solution.py:299
  102.9 0.2 convert_reduce_fusion
  103.1 0.1 copy.19
  103.2 0.7 copy.20
  (2 shorter events, 0.0 us)
Async XLA Ops:
  3.3 23.9 %all-to-all-start = ((bf16[128,16,128]{2,1,0:T(8,128)(2,1)}), bf16[128,16,128]{2,1,0:T(8,128)(2,1)S(1)}, u32[]{:S(2)}, u32[]{:S(2)}) async-start(bf16[128,16,128]{2,1,0:T(8,128)(2,1)} %broadcast_in_dim.39), calls=%async_computation | async-start | bytes 1048576 | tf_op jit(solution)/shard_map/all_to_all | solution.py:319
  27.2 22.0 %copy-start = (f32[8]{0:T(128)S(1)}, f32[8]{0:T(128)}, u32[]{:S(2)}) copy-start(f32[8]{0:T(128)} %table.3) | copy-start | bytes 100
  41.9 7.3 %collective-permute-start.4 = (bf16[3,272,128]{2,1,0:T(8,128)(2,1)S(1)}, bf16[3,272,128]{2,1,0:T(8,128)(2,1)S(1)}, u32[]{:S(2)}, u32[]{:S(2)}) collective-permute-start(bf16[3,272,128]{2,1,0:T(8,128)(2,1)S(1)} %get-tuple-element.23), channel_id=1, source_target_pairs={{0,16},{16,0},{32,48},{48,32},{64,80},{80,64},{96,112},{112,96},{1... | collective-permute-start | bytes 626696 | tf_op jit(solution)/shard_map/ppermute | solution.py:306
  42.0 7.2 %collective-permute-start.5 = (bf16[3,272,128]{2,1,0:T(8,128)(2,1)S(1)}, bf16[3,272,128]{2,1,0:T(8,128)(2,1)S(1)}, u32[]{:S(2)}, u32[]{:S(2)}) collective-permute-start(bf16[3,272,128]{2,1,0:T(8,128)(2,1)S(1)} %get-tuple-element.24), channel_id=1, source_target_pairs={{16,32},{48,64},{80,96},{32,16},{64,48},{96,80},{17,33},{49,65},{8... | collective-permute-start | bytes 626696 | tf_op jit(solution)/shard_map/ppermute | solution.py:307
  42.7 1.3 %collective-permute-start = (bf16[16,16,128]{2,1,0:T(8,128)(2,1)S(1)}, bf16[16,16,128]{2,1,0:T(8,128)(2,1)S(1)}, u32[]{:S(2)}, u32[]{:S(2)}) collective-permute-start(bf16[16,16,128]{2,1,0:T(8,128)(2,1)S(1)} %get-tuple-element.17), channel_id=1, source_target_pairs={{0,1},{1,0},{2,3},{3,2},{4,5},{5,4},{6,7},{7,6},{8,9},{9,8},{10,11... | collective-permute-start | bytes 196616 | tf_op jit(solution)/shard_map/ppermute | solution.py:306
  42.9 1.1 %collective-permute-start.1 = (bf16[16,16,128]{2,1,0:T(8,128)(2,1)S(1)}, bf16[16,16,128]{2,1,0:T(8,128)(2,1)S(1)}, u32[]{:S(2)}, u32[]{:S(2)}) collective-permute-start(bf16[16,16,128]{2,1,0:T(8,128)(2,1)S(1)} %get-tuple-element.18), channel_id=1, source_target_pairs={{1,2},{3,4},{5,6},{7,8},{9,10},{11,12},{13,14},{2,1},{4,3},{6,5},{... | collective-permute-start | bytes 196616 | tf_op jit(solution)/shard_map/ppermute | solution.py:307
  44.2 10.8 %collective-permute-start.2 = (bf16[3,80,128]{2,1,0:T(8,128)(2,1)S(1)}, bf16[3,80,128]{2,1,0:T(8,128)(2,1)S(1)}, u32[]{:S(2)}, u32[]{:S(2)}) collective-permute-start(bf16[3,80,128]{2,1,0:T(8,128)(2,1)S(1)} %get-tuple-element.20), channel_id=1, source_target_pairs={{0,16},{16,0},{32,48},{48,32},{64,80},{80,64},{96,112},{112,96},{1... | collective-permute-start | bytes 184328 | tf_op jit(solution)/shard_map/ppermute | solution.py:306
  48.3 6.7 %collective-permute-start.3 = (bf16[3,80,128]{2,1,0:T(8,128)(2,1)S(1)}, bf16[3,80,128]{2,1,0:T(8,128)(2,1)S(1)}, u32[]{:S(2)}, u32[]{:S(2)}) collective-permute-start(bf16[3,80,128]{2,1,0:T(8,128)(2,1)S(1)} %get-tuple-element.21), channel_id=1, source_target_pairs={{16,32},{48,64},{80,96},{32,16},{64,48},{96,80},{17,33},{49,65},{8... | collective-permute-start | bytes 184328 | tf_op jit(solution)/shard_map/ppermute | solution.py:307
  63.9 8.7 %collective-permute-start.6 = (bf16[64,16,512]{2,1,0:T(8,128)(2,1)S(1)}, bf16[64,16,512]{2,1,0:T(8,128)(2,1)S(1)}, u32[]{:S(2)}, u32[]{:S(2)}) collective-permute-start(bf16[64,16,512]{2,1,0:T(8,128)(2,1)S(1)} %get-tuple-element.28), channel_id=1, source_target_pairs={{0,1},{1,0},{2,3},{3,2},{4,5},{5,4},{6,7},{7,6},{8,9},{9,8},{10,11... | collective-permute-start | bytes 3145736 | tf_op jit(solution)/shard_map/ppermute | solution.py:297

commit v4 on v3

--- a/solution.py
+++ b/solution.py
@@ -1,9 +1,12 @@
+import functools
+
 import jax
 import jax.numpy as jnp
 from jax import lax
 from jax.experimental import pallas as pl
 from jax.experimental.pallas import tpu as pltpu
 from jax.sharding import PartitionSpec as P
+
 
 SWEEPS = 3
 WIDE, NARROW = ("z_lo", "x"), ("y", "z_hi", "core")
@@ -22,6 +25,31 @@
     return pltpu.CompilerParams(vmem_limit_bytes=mib << 20)
 
 
+def choose_body(column_freq, data, out):
+    own = data.shape[2]
+    narrow = (lax.axis_index("y") * 2 + lax.axis_index("z_hi")) * 2 + lax.axis_index("core")
+    shape = (own, 2 * data.shape[3])
+    column = lax.broadcasted_iota(jnp.int32, shape, 0)
+    freq = jnp.zeros(shape, jnp.int32)
+    for j in range(own):
+        freq = jnp.where(column == j, column_freq[narrow * own + j], freq)
+    block = jnp.zeros(shape, F32)
+    for f in range(FREQ):
+        both = jnp.concatenate([data[f, 0], data[f, 1]], axis=1).astype(F32)
+        block = jnp.where(freq == f, both, block)
+    out[...] = jnp.broadcast_to(block.astype(BF16)[None], out.shape)
+
+
+def choose(column_freq, data, receivers):
+    return pl.pallas_call(
+        choose_body,
+        in_specs=[SCALARS, WHOLE],
+        out_specs=pl.BlockSpec(),
+        out_shape=jax.ShapeDtypeStruct((receivers, data.shape[2], 2 * data.shape[3]), BF16),
+        compiler_params=params(8),
+    )(column_freq, data)
+
+
 def strip_lane(rows):
     left = (rows >= 3) & (rows < 12)
     right = (rows >= 12) & (rows < 21)
@@ -30,12 +58,12 @@
 
 def adjoint_body(inv, gathered, freq, stored, classes, ops, field, strips, y_a, y_b, x_a, x_b, buf, sems, probes):
     group = pl.program_id(0)
-    per = buf.shape[2]
+    per = buf.shape[3]
 
     def fetch(which, slot):
         def one(j, _):
             sensor = inv[which * per + j]
-            pltpu.make_async_copy(stored.at[sensor], buf.at[slot, :, j], sems.at[slot]).start()
+            pltpu.make_async_copy(stored.at[sensor], buf.at[slot, :, :, j], sems.at[slot]).start()
             return 0
 
         lax.fori_loop(0, per, one, 0, unroll=8)
@@ -114,7 +142,7 @@
             x_edge,
         ),
         scratch_shapes=[
-            pltpu.VMEM((2, FREQ, per, 2, PX, PY), BF16),
+            pltpu.VMEM((2, FREQ, 2, per, PX, PY), BF16),
             pltpu.SemaphoreType.DMA((2,)),
             pltpu.VMEM((COLS, KW), BF16),
         ],
@@ -293,29 +321,44 @@
     )(prior, ops)
 
 
-def reduced(keep, send):
+def total_body(pieces, out, *, weight):
+    total = pieces[0].astype(F32)
+    for chip in range(1, pieces.shape[0]):
+        total = total + pieces[chip].astype(F32)
+    total = (total * weight).astype(BF16)
+    rows = out.shape[3]
+    for f in range(FREQ):
+        for q in range(2):
+            at = (f * 2 + q) * rows
+            out[f, q] = total[:, at : at + rows]
+
+
+def reduced(keep, send, weight):
     got = lax.ppermute(send, "core", [(0, 1), (1, 0)])
     chip = (keep + got.astype(F32)).astype(BF16)
     pieces = lax.all_to_all(chip, CHIPS, 0, 0, tiled=True)
-    return jnp.sum(pieces.astype(F32), axis=0)
+    return pl.pallas_call(
+        functools.partial(total_body, weight=weight),
+        in_specs=[WHOLE],
+        out_specs=pl.BlockSpec(),
+        out_shape=jax.ShapeDtypeStruct((FREQ, 2, pieces.shape[1], KW // (FREQ * 2)), BF16),
+        compiler_params=params(8),
+    )(pieces)
 
 
 def swapped(first, second, axis):
     size = lax.axis_size(axis)
     odd = [(i, i + 1) for i in range(1, size - 1, 2)]
-    got = lax.ppermute(first, axis, [(i, i ^ 1) for i in range(size)])
-    return got, lax.ppermute(second, axis, odd + [(j, i) for i, j in odd])
+    far = lax.ppermute(second, axis, odd + [(j, i) for i, j in odd])
+    near = lax.ppermute(first, axis, [(i, i ^ 1) for i in range(size)])
+    return near, far
 
 
 def on_device(seafloor_ops, sensor_data, column_freq, row_owner, coef_class, coef_table):
     sens = seafloor_ops.shape[0]
-    per, own = sensor_data.shape[0], sensor_data.shape[3]
+    per = sensor_data.shape[0]
     quad_weight = 2.0 * sens / (PX * lax.axis_size(WIDE) * PY * lax.axis_size(NARROW))
-    my_freq = lax.dynamic_slice_in_dim(column_freq, lax.axis_index(NARROW) * own, own)
-    mask = my_freq[None, None, None, :] == jnp.arange(FREQ, dtype=jnp.int32)[None, :, None, None]
-    chosen = jnp.sum(jnp.where(mask, sensor_data, 0).astype(F32), axis=1).astype(BF16)
-    block = chosen.reshape(per * 2, own).T
-    sent = jnp.broadcast_to(block[None], (128,) + block.shape)
+    sent = choose(column_freq, sensor_data.transpose(1, 2, 3, 0), lax.axis_size(BOTH))
     gathered = lax.all_to_all(sent, BOTH, 0, 0, tiled=True).reshape(NW, COLS, per * 2)
 
     ids = jnp.arange(sens, dtype=jnp.int32)
@@ -331,8 +374,7 @@
     s_a, s_b = swapped(s_a, s_b, WIDE)
     inner = inner_sweeps(coef_table, field, x_a, x_b, classes)
     prior, prior_field = outer_sweeps(coef_table, whole, s_a, s_b, inner)
-    total = reduced(*forward(prior, ops)) * quad_weight
-    hessian = total.astype(BF16).reshape(own, FREQ, per, 2).transpose(2, 1, 3, 0)
+    hessian = reduced(*forward(prior, ops), quad_weight).transpose(3, 0, 1, 2)
     return hessian, prior_field
 
 

time: 104 us -> 104 us (level)
  Pallas kernels: 29.5 us -> 31.8 us
  local copies, waits for them, and re-layouts: 3.47 us -> 2.24 us
    pallas_call x0 -> x2, Pallas kernels: none -> 2.31 us  [the longest x1 1.45 us: choose(): pl.pallas_call(choose_body, in_specs=[SCALARS, WHOLE], out_specs=pl.Block...]
where the time goes in v4:
time: 104 us
  Pallas kernels  31.8 us (31%)
  blocking collectives  29.9 us (29%)
  starting transfers between devices  23.9 us (23%)
  waiting for transfers between devices  13.4 us (13%)
  local copies, waits for them, and re-layouts  2.24 us (2%)
  other arithmetic  1.97 us (2%)
    all_to_all x1, blocking collectives, reduced(): pieces = lax.all_to_all(chip, CHIPS, 0, 0, tiled=True)  29.9 us
    pallas_call x1, Pallas kernels, adjoint(): pl.pallas_call(adjoint_body, grid=(NW,), in_specs=[SCALARS, WHOLE, WHOLE,...  14.7 us
    all_to_all x1, starting transfers between devices, on_device(): lax.all_to_all(sent, BOTH, 0, 0, tiled=True).reshape(NW, COLS, per * 2)  11.2 us
    all_to_all x1, waiting for transfers between devices, on_device(): lax.all_to_all(sent, BOTH, 0, 0, tiled=True).reshape(NW, COLS, per * 2)  10.4 us
    ppermute x1, starting transfers between devices, reduced(): got = lax.ppermute(send, 'core', [(0, 1), (1, 0)])  6.37 us
    pallas_call x1, Pallas kernels, forward(): pl.pallas_call(forward_body, grid=(NW,), in_specs=[WHOLE, WHOLE], out_spe...  6.02 us
    pallas_call x1, Pallas kernels, inner_sweeps(): pl.pallas_call(inner_body, in_specs=[SCALARS] + [WHOLE] * 4, out_specs=WH...  5.73 us
    ppermute x3, starting transfers between devices, swapped(): near = lax.ppermute(first, axis, [(i, i ^ 1) for i in range(size)])  4.42 us
  transfers between devices with their start and end apart: 8, of which 4 were waited for; matrix products, arithmetic and copies ran while one was open for 2% of the time, Pallas kernels for 6%

profile of v4, /device:TPU:0, one launch (start us, length us, event | category | flops | bytes accessed | tf_op | source)
XLA Modules:
  0.0 104.0 jit_solution(5788600708485721447)
XLA Ops:
  0.6 0.0 copy-start
  0.6 0.7 copy-done
  1.4 0.0 copy-start.1
  1.4 0.7 copy-done.1
  2.1 1.4 %shard_map.77 = bf16[128,16,128]{2,1,0:T(8,128)(2,1)} custom-call(s32[256]{0:T(256)S(1)} %copy-done.1, bf16[4,2,16,64]{3,2,1,0:T(8,128)(2,1)S(1)} %bitcast.5), custom_call_target="tpu_custom_call" | custom-call | tf_op jit(solution)/shard_map/pallas_call | solution.py:44
  3.5 11.2 %all-to-all-start = ((bf16[128,16,128]{2,1,0:T(8,128)(2,1)}), bf16[128,16,128]{2,1,0:T(8,128)(2,1)S(1)}, u32[]{:S(2)}, u32[]{:S(2)}) async-start(bf16[128,16,128]{2,1,0:T(8,128)(2,1)} %shard_map.77), calls=%async_computation | async-start | bytes 1048576 | tf_op jit(solution)/shard_map/all_to_all | solution.py:362
  14.7 0.8 copy.9.freq
  15.5 0.9 select_reduce_fusion.inv
  16.4 0.7 add_convert_fusion.1.classes
  17.1 10.4 %all-to-all-done = bf16[128,16,128]{2,1,0:T(8,128)(2,1)S(1)} async-done(((bf16[128,16,128]{2,1,0:T(8,128)(2,1)}), bf16[128,16,128]{2,1,0:T(8,128)(2,1)S(1)}, u32[]{:S(2)}, u32[]{:S(2)}) %all-to-all-start) | async-done | bytes 524320 | tf_op jit(solution)/shard_map/all_to_all | solution.py:362
  27.4 0.0 copy-start.2
  27.4 14.7 %shard_map.78 = (bf16[16,4096,128]{2,1,0:T(8,128)(2,1)S(1)}, f32[16,256,128]{2,1,0:T(8,128)S(1)}, f32[16,3,24,128]{3,2,1,0:T(8,128)S(1)}, bf16[16,16,128]{2,1,0:...) custom-call(s32[512]{0:T(512)S(1)} %select_reduce_fusion.inv, ...), custom_call_target="tpu_custom_call" | custom-call | tf_op jit(solution)/shard_map/pallas_call | solution.py:130
  42.2 0.1 collective-permute-start.4
  42.3 0.7 collective-permute-start.5
  42.9 0.2 collective-permute-start
  43.1 0.7 collective-permute-start.1
  43.8 0.5 collective-permute-done.y_a
  44.3 0.0 collective-permute-done.1.y_b
  44.3 0.1 shard_map.79
  44.4 4.1 %collective-permute-start.2 = (bf16[3,80,128]{2,1,0:T(8,128)(2,1)S(1)}, bf16[3,80,128]{2,1,0:T(8,128)(2,1)S(1)}, u32[]{:S(2)}, u32[]{:S(2)}) collective-permute-start(bf16[3,80,128]{2,1,0:T(8,128)(2,1)S(1)} %get-tuple-element.20), channel_id=1, source_target_pairs={{0,16},{16,0},{32,48},{48,32},{64,80},{80,64},{96,112},{112,96},{1... | collective-permute-start | bytes 184328 | tf_op jit(solution)/shard_map/ppermute | solution.py:353
  48.5 0.7 collective-permute-start.3
  49.2 0.2 collective-permute-done.4.x_a
  49.4 0.0 collective-permute-done.5.x_b
  49.4 0.0 copy-done.2
  49.4 5.7 %shard_map.80.inner = bf16[16,256,128]{2,1,0:T(8,128)(2,1)S(1)} custom-call(f32[8]{0:T(128)S(1)} %copy-done.2, f32[16,256,128]{2,1,0:T(8,128)S(1)} %get-tuple-element.22.field, bf16[3,272,128]{2,1,0:T(8,128)(2,1)S(1)} %collective-permute-done.4.x_a, bf16[3,272,128]{2,1,0:T(8,128)(2,1)S(1)} %collective-permute-done.5.x_b, f32[16,128]{1,0:T(8,128)S(1)} %add_convert_fusion.1.classes), custom_call_target="tpu_custom_call" | custom-call | tf_op jit(solution)/shard_map/pallas_call | solution.py:248
  55.2 0.0 collective-permute-done.2.s_a
  55.2 0.0 collective-permute-done.3.s_b
  55.2 2.9 %shard_map.81 = (bf16[16,256,128]{2,1,0:T(8,128)(2,1)S(1)}, bf16[256,16,128]{2,1,0:T(8,128)(2,1)}) custom-call(f32[8]{0:T(128)S(1)} %copy-done.2, f32[16,3,24,128]{3,2,1,0:T(8,128)S(1)} %get-tuple-element.19.whole, bf16[3,80,128]{2,1,0:T(8,128)(2,1)S(1)} %collective-permute-done.2.s_a, bf16[3,80,128]{2,1,0:T(8,128)(2,1)S(1)} %collective-permute-done.3.s_b, ...), custom_call_target="tpu_custom_call" | custom-call | tf_op jit(solution)/shard_map/pallas_call | solution.py:282
  58.1 6.0 %shard_map.82 = (f32[64,16,512]{2,1,0:T(8,128)S(1)}, bf16[64,16,512]{2,1,0:T(8,128)(2,1)S(1)}) custom-call(bf16[16,256,128]{2,1,0:T(8,128)(2,1)S(1)} %get-tuple-element.25.prior, bf16[16,4096,128]{2,1,0:T(8,128)(2,1)S(1)} %get-tuple-element.26.ops), custom_call_target="tpu_custom_call" | custom-call | tf_op jit(solution)/shard_map/pallas_call | solution.py:311
  64.1 6.4 %collective-permute-start.6 = (bf16[64,16,512]{2,1,0:T(8,128)(2,1)S(1)}, bf16[64,16,512]{2,1,0:T(8,128)(2,1)S(1)}, u32[]{:S(2)}, u32[]{:S(2)}) collective-permute-start(bf16[64,16,512]{2,1,0:T(8,128)(2,1)S(1)} %get-tuple-element.28), channel_id=1, source_target_pairs={{0,1},{1,0},{2,3},{3,2},{4,5},{5,4},{6,7},{7,6},{8,9},{9,8},{10,11... | collective-permute-start | bytes 3145736 | tf_op jit(solution)/shard_map/ppermute | solution.py:337
  70.5 2.3 %collective-permute-done.6 = bf16[64,16,512]{2,1,0:T(8,128)(2,1)S(1)} collective-permute-done((bf16[64,16,512]{2,1,0:T(8,128)(2,1)S(1)}, bf16[64,16,512]{2,1,0:T(8,128)(2,1)S(1)}, u32[]{:S(2)}, u32[]{:S(2)}) %collective-permute-start.6) | collective-permute-done | bytes 1048608 | tf_op jit(solution)/shard_map/ppermute | solution.py:337
  72.8 0.4 add_convert_fusion
  73.2 29.9 %all_to_all.10.pieces = bf16[64,16,512]{2,1,0:T(8,128)(2,1)S(1)} all-to-all(bf16[64,16,512]{2,1,0:T(8,128)(2,1)S(1)} %add_convert_fusion), channel_id=1, replica_groups=mesh['z_lo'=2,'x'=4,'y'=4,'z_hi'=2,'core'=2] {'z_lo','x','y','z_hi'}, dimensions={0} | all-to-all | bytes 2097152 | tf_op jit(solution)/shard_map/all_to_all | solution.py:339
  103.1 0.9 shard_map.83
Async XLA Ops:
  0.6 0.8 copy-start
  1.4 0.7 copy-start.1
  3.5 23.9 %all-to-all-start = ((bf16[128,16,128]{2,1,0:T(8,128)(2,1)}), bf16[128,16,128]{2,1,0:T(8,128)(2,1)S(1)}, u32[]{:S(2)}, u32[]{:S(2)}) async-start(bf16[128,16,128]{2,1,0:T(8,128)(2,1)} %shard_map.77), calls=%async_computation | async-start | bytes 1048576 | tf_op jit(solution)/shard_map/all_to_all | solution.py:362
  27.4 22.0 %copy-start.2 = (f32[8]{0:T(128)S(1)}, f32[8]{0:T(128)}, u32[]{:S(2)}) copy-start(f32[8]{0:T(128)} %table.3) | copy-start | bytes 100
  42.2 7.3 %collective-permute-start.4 = (bf16[3,272,128]{2,1,0:T(8,128)(2,1)S(1)}, bf16[3,272,128]{2,1,0:T(8,128)(2,1)S(1)}, u32[]{:S(2)}, u32[]{:S(2)}) collective-permute-start(bf16[3,272,128]{2,1,0:T(8,128)(2,1)S(1)} %get-tuple-element.23), channel_id=1, source_target_pairs={{0,16},{16,0},{32,48},{48,32},{64,80},{80,64},{96,112},{112,96},{1... | collective-permute-start | bytes 626696 | tf_op jit(solution)/shard_map/ppermute | solution.py:353
  42.3 7.2 %collective-permute-start.5 = (bf16[3,272,128]{2,1,0:T(8,128)(2,1)S(1)}, bf16[3,272,128]{2,1,0:T(8,128)(2,1)S(1)}, u32[]{:S(2)}, u32[]{:S(2)}) collective-permute-start(bf16[3,272,128]{2,1,0:T(8,128)(2,1)S(1)} %get-tuple-element.24), channel_id=1, source_target_pairs={{16,32},{48,64},{80,96},{32,16},{64,48},{96,80},{17,33},{49,65},{8... | collective-permute-start | bytes 626696 | tf_op jit(solution)/shard_map/ppermute | solution.py:352
  42.9 1.3 %collective-permute-start = (bf16[16,16,128]{2,1,0:T(8,128)(2,1)S(1)}, bf16[16,16,128]{2,1,0:T(8,128)(2,1)S(1)}, u32[]{:S(2)}, u32[]{:S(2)}) collective-permute-start(bf16[16,16,128]{2,1,0:T(8,128)(2,1)S(1)} %get-tuple-element.17), channel_id=1, source_target_pairs={{0,1},{1,0},{2,3},{3,2},{4,5},{5,4},{6,7},{7,6},{8,9},{9,8},{10,11... | collective-permute-start | bytes 196616 | tf_op jit(solution)/shard_map/ppermute | solution.py:353
  43.1 1.1 %collective-permute-start.1 = (bf16[16,16,128]{2,1,0:T(8,128)(2,1)S(1)}, bf16[16,16,128]{2,1,0:T(8,128)(2,1)S(1)}, u32[]{:S(2)}, u32[]{:S(2)}) collective-permute-start(bf16[16,16,128]{2,1,0:T(8,128)(2,1)S(1)} %get-tuple-element.18), channel_id=1, source_target_pairs={{1,2},{3,4},{5,6},{7,8},{9,10},{11,12},{13,14},{2,1},{4,3},{6,5},{... | collective-permute-start | bytes 196616 | tf_op jit(solution)/shard_map/ppermute | solution.py:352
  44.4 10.8 %collective-permute-start.2 = (bf16[3,80,128]{2,1,0:T(8,128)(2,1)S(1)}, bf16[3,80,128]{2,1,0:T(8,128)(2,1)S(1)}, u32[]{:S(2)}, u32[]{:S(2)}) collective-permute-start(bf16[3,80,128]{2,1,0:T(8,128)(2,1)S(1)} %get-tuple-element.20), channel_id=1, source_target_pairs={{0,16},{16,0},{32,48},{48,32},{64,80},{80,64},{96,112},{112,96},{1... | collective-permute-start | bytes 184328 | tf_op jit(solution)/shard_map/ppermute | solution.py:353
  48.5 6.7 %collective-permute-start.3 = (bf16[3,80,128]{2,1,0:T(8,128)(2,1)S(1)}, bf16[3,80,128]{2,1,0:T(8,128)(2,1)S(1)}, u32[]{:S(2)}, u32[]{:S(2)}) collective-permute-start(bf16[3,80,128]{2,1,0:T(8,128)(2,1)S(1)} %get-tuple-element.21), channel_id=1, source_target_pairs={{16,32},{48,64},{80,96},{32,16},{64,48},{96,80},{17,33},{49,65},{8... | collective-permute-start | bytes 184328 | tf_op jit(solution)/shard_map/ppermute | solution.py:352
  64.1 8.7 %collective-permute-start.6 = (bf16[64,16,512]{2,1,0:T(8,128)(2,1)S(1)}, bf16[64,16,512]{2,1,0:T(8,128)(2,1)S(1)}, u32[]{:S(2)}, u32[]{:S(2)}) collective-permute-start(bf16[64,16,512]{2,1,0:T(8,128)(2,1)S(1)} %get-tuple-element.28), channel_id=1, source_target_pairs={{0,1},{1,0},{2,3},{3,2},{4,5},{5,4},{6,7},{7,6},{8,9},{9,8},{10,11... | collective-permute-start | bytes 3145736 | tf_op jit(solution)/shard_map/ppermute | solution.py:337

commit v5 on v4

--- a/solution.py
+++ b/solution.py
@@ -56,7 +56,7 @@
     return jnp.where(left, rows - 3, jnp.where(right, rows + (PY - 21), -1))
 
 
-def adjoint_body(inv, gathered, freq, stored, classes, ops, field, strips, y_a, y_b, x_a, x_b, buf, sems, probes):
+def adjoint_body(inv, gathered, freq, stored, classes, ops, field, strips, y_a, y_b, x_a, x_b, buf, sems, probes, masks):
     group = pl.program_id(0)
     per = buf.shape[3]
 
@@ -72,6 +72,8 @@
     def _():
         fetch(0, 0)
         field[...] = jnp.zeros_like(field)
+        for f in range(FREQ):
+            masks[f] = jnp.broadcast_to((freq[...] == f).astype(F32), (COLS, 128)).astype(BF16)
 
     @pl.when(group + 1 < pl.num_programs(0))
     def _():
@@ -80,7 +82,7 @@
     slot = group % 2
     block = gathered[group]
     for f in range(FREQ):
-        probes[:, f * 128 : f * 128 + 128] = jnp.where(freq[...] == f, block, 0).astype(BF16)
+        probes[:, f * 128 : f * 128 + 128] = block * masks[f]
     pltpu.make_async_copy(buf.at[slot], buf.at[slot], sems.at[slot]).wait()
     for f in range(0, FREQ, 2):
         laid = jnp.swapaxes(buf[slot, f : f + 2].reshape(per * 4, PX, PY), 0, 1)
@@ -145,6 +147,7 @@
             pltpu.VMEM((2, FREQ, 2, per, PX, PY), BF16),
             pltpu.SemaphoreType.DMA((2,)),
             pltpu.VMEM((COLS, KW), BF16),
+            pltpu.VMEM((FREQ, COLS, 128), BF16),
         ],
         compiler_params=params(24),
     )(inv, gathered, freq, stored, classes)
@@ -255,7 +258,7 @@
     )(table, field, x_a, x_b, classes)
 
 
-def outer_body(table, whole, s_a, s_b, inner, prior, prior_out, coef):
+def outer_body(table, whole, s_a, s_b, inner, prior, coef):
     even = lax.axis_index(WIDE[-1]) % 2 == 0
 
     def strip_rows(t):
@@ -275,24 +278,20 @@
         both = jnp.concatenate([edge[0][x], edge[1][x]], axis=1).astype(BF16)
         at_edge = lax.dot_general(both, pick, tn, preferred_element_type=F32)
         prior[x] = jnp.where(middle, inner[x].astype(F32), at_edge).astype(BF16)
-    prior_out[...] = jnp.swapaxes(prior[...], 0, 1)
 
 
 def outer_sweeps(table, whole, s_a, s_b, inner):
     return pl.pallas_call(
         outer_body,
         in_specs=[SCALARS] + [WHOLE] * 4,
-        out_specs=(WHOLE, pl.BlockSpec()),
-        out_shape=(
-            jax.ShapeDtypeStruct((PX, COLS, PY), BF16),
-            jax.ShapeDtypeStruct((COLS, PX, PY), BF16),
-        ),
+        out_specs=WHOLE,
+        out_shape=jax.ShapeDtypeStruct((PX, COLS, PY), BF16),
         scratch_shapes=[pltpu.VMEM((PX + 6, 5, STRIP, PY), F32)],
         compiler_params=params(12),
     )(table, whole, s_a, s_b, inner)
 
 
-def forward_body(prior, ops, keep, send):
+def forward_body(prior, ops, keep, send, prior_out):
     group = pl.program_id(0)
     core = lax.axis_index("core")
     rows = pl.ds(pl.multiple_of(group * KW, KW), KW)
@@ -300,6 +299,9 @@
     right = jnp.concatenate([ops[x, rows, :] for x in range(PX)], axis=1)
     nt = (((1,), (1,)), ((), ()))
     total = lax.dot_general(left, right, nt, preferred_element_type=F32)
+    own = prior_out.shape[0]
+    columns = pl.ds(pl.multiple_of(group * own, own), own)
+    prior_out[...] = jnp.swapaxes(prior[:, columns, :], 0, 1)
     for chip in range(8):
         even = total[chip * 32 : chip * 32 + 16]
         odd = total[chip * 32 + 16 : chip * 32 + 32]
@@ -312,10 +314,11 @@
         forward_body,
         grid=(NW,),
         in_specs=[WHOLE, WHOLE],
-        out_specs=(WHOLE, WHOLE),
+        out_specs=(WHOLE, WHOLE, pl.BlockSpec((COLS // NW, PX, PY), lambda i: (i, 0, 0))),
         out_shape=(
             jax.ShapeDtypeStruct((64, 16, KW), F32),
             jax.ShapeDtypeStruct((64, 16, KW), BF16),
+            jax.ShapeDtypeStruct((COLS, PX, PY), BF16),
         ),
         compiler_params=params(16),
     )(prior, ops)
@@ -373,8 +376,9 @@
     whole, s_a, s_b = edges(strips, y_a, y_b)
     s_a, s_b = swapped(s_a, s_b, WIDE)
     inner = inner_sweeps(coef_table, field, x_a, x_b, classes)
-    prior, prior_field = outer_sweeps(coef_table, whole, s_a, s_b, inner)
-    hessian = reduced(*forward(prior, ops), quad_weight).transpose(3, 0, 1, 2)
+    prior = outer_sweeps(coef_table, whole, s_a, s_b, inner)
+    keep, send, prior_field = forward(prior, ops)
+    hessian = reduced(keep, send, quad_weight).transpose(3, 0, 1, 2)
     return hessian, prior_field
 
 

time: 104 us -> 103 us (level)
  Pallas kernels: 31.8 us -> 30.1 us
    pallas_call x1, Pallas kernels: 14.7 us -> 13.5 us  [adjoint(): pl.pallas_call(adjoint_body, grid=(NW,), in_specs=[SCALARS, WHOLE, WHOLE,...]
    pallas_call x1, Pallas kernels: 2.91 us -> 1.81 us  [outer_sweeps(): pl.pallas_call(outer_body, in_specs=[SCALARS] + [WHOLE] * 4, out_specs=WH...]
where the time goes in v5:
time: 103 us; the launch traced here: 102 us
  Pallas kernels  30.1 us (29%)
  blocking collectives  29.9 us (29%)
  starting transfers between devices  23.8 us (23%)
  waiting for transfers between devices  13.4 us (13%)
  local copies, waits for them, and re-layouts  2.24 us (2%)
  other arithmetic  1.97 us (2%)
    all_to_all x1, blocking collectives, reduced(): pieces = lax.all_to_all(chip, CHIPS, 0, 0, tiled=True)  29.9 us
    pallas_call x1, Pallas kernels, adjoint(): pl.pallas_call(adjoint_body, grid=(NW,), in_specs=[SCALARS, WHOLE, WHOLE,...  13.5 us
    all_to_all x1, starting transfers between devices, on_device(): lax.all_to_all(sent, BOTH, 0, 0, tiled=True).reshape(NW, COLS, per * 2)  11.2 us
    all_to_all x1, waiting for transfers between devices, on_device(): lax.all_to_all(sent, BOTH, 0, 0, tiled=True).reshape(NW, COLS, per * 2)  10.4 us
    pallas_call x1, Pallas kernels, forward(): pl.pallas_call(forward_body, grid=(NW,), in_specs=[WHOLE, WHOLE], out_spe...  6.69 us
    ppermute x1, starting transfers between devices, reduced(): got = lax.ppermute(send, 'core', [(0, 1), (1, 0)])  6.28 us
    pallas_call x1, Pallas kernels, inner_sweeps(): pl.pallas_call(inner_body, in_specs=[SCALARS] + [WHOLE] * 4, out_specs=WH...  5.71 us
    ppermute x3, starting transfers between devices, swapped(): near = lax.ppermute(first, axis, [(i, i ^ 1) for i in range(size)])  4.42 us
  transfers between devices with their start and end apart: 8, of which 4 were waited for; matrix products, arithmetic and copies ran while one was open for 2% of the time, Pallas kernels for 6%

profile of v5, /device:TPU:0, one launch (start us, length us, event | category | flops | bytes accessed | tf_op | source)
XLA Modules:
  0.0 102.2 jit_solution(15470313555538859826)
XLA Ops:
  0.6 0.0 copy-start
  0.6 0.7 copy-done
  1.4 0.0 copy-start.1
  1.4 0.7 copy-done.1
  2.1 1.4 %shard_map.77 = bf16[128,16,128]{2,1,0:T(8,128)(2,1)} custom-call(s32[256]{0:T(256)S(1)} %copy-done.1, bf16[4,2,16,64]{3,2,1,0:T(8,128)(2,1)S(1)} %bitcast.5), custom_call_target="tpu_custom_call" | custom-call | tf_op jit(solution)/shard_map/pallas_call | solution.py:44
  3.5 11.2 %all-to-all-start = ((bf16[128,16,128]{2,1,0:T(8,128)(2,1)}), bf16[128,16,128]{2,1,0:T(8,128)(2,1)S(1)}, u32[]{:S(2)}, u32[]{:S(2)}) async-start(bf16[128,16,128]{2,1,0:T(8,128)(2,1)} %shard_map.77), calls=%async_computation | async-start | bytes 1048576 | tf_op jit(solution)/shard_map/all_to_all | solution.py:365
  14.7 0.8 copy.9.freq
  15.5 0.9 select_reduce_fusion.inv
  16.4 0.7 add_convert_fusion.1.classes
  17.1 10.4 %all-to-all-done = bf16[128,16,128]{2,1,0:T(8,128)(2,1)S(1)} async-done(((bf16[128,16,128]{2,1,0:T(8,128)(2,1)}), bf16[128,16,128]{2,1,0:T(8,128)(2,1)S(1)}, u32[]{:S(2)}, u32[]{:S(2)}) %all-to-all-start) | async-done | bytes 524320 | tf_op jit(solution)/shard_map/all_to_all | solution.py:365
  27.4 0.0 copy-start.2
  27.4 13.5 %shard_map.78 = (bf16[16,4096,128]{2,1,0:T(8,128)(2,1)S(1)}, f32[16,256,128]{2,1,0:T(8,128)S(1)}, f32[16,3,24,128]{3,2,1,0:T(8,128)S(1)}, bf16[16,16,128]{2,1,0:...) custom-call(s32[512]{0:T(512)S(1)} %select_reduce_fusion.inv, ...), custom_call_target="tpu_custom_call" | custom-call | tf_op jit(solution)/shard_map/pallas_call | solution.py:132
  40.9 0.1 collective-permute-start.4
  41.0 0.7 collective-permute-start.5
  41.7 0.2 collective-permute-start
  41.9 0.7 collective-permute-start.1
  42.5 0.5 collective-permute-done.y_a
  43.0 0.0 collective-permute-done.1.y_b
  43.0 0.1 shard_map.79
  43.1 4.1 %collective-permute-start.2 = (bf16[3,80,128]{2,1,0:T(8,128)(2,1)S(1)}, bf16[3,80,128]{2,1,0:T(8,128)(2,1)S(1)}, u32[]{:S(2)}, u32[]{:S(2)}) collective-permute-start(bf16[3,80,128]{2,1,0:T(8,128)(2,1)S(1)} %get-tuple-element.19), channel_id=1, source_target_pairs={{0,16},{16,0},{32,48},{48,32},{64,80},{80,64},{96,112},{112,96},{1... | collective-permute-start | bytes 184328 | tf_op jit(solution)/shard_map/ppermute | solution.py:356
  47.3 0.7 collective-permute-start.3
  47.9 0.2 collective-permute-done.4.x_a
  48.2 0.0 collective-permute-done.5.x_b
  48.2 0.0 copy-done.2
  48.2 5.7 %shard_map.80.inner = bf16[16,256,128]{2,1,0:T(8,128)(2,1)S(1)} custom-call(f32[8]{0:T(128)S(1)} %copy-done.2, f32[16,256,128]{2,1,0:T(8,128)S(1)} %get-tuple-element.21.field, bf16[3,272,128]{2,1,0:T(8,128)(2,1)S(1)} %collective-permute-done.4.x_a, bf16[3,272,128]{2,1,0:T(8,128)(2,1)S(1)} %collective-permute-done.5.x_b, f32[16,128]{1,0:T(8,128)S(1)} %add_convert_fusion.1.classes), custom_call_target="tpu_custom_call" | custom-call | tf_op jit(solution)/shard_map/pallas_call | solution.py:251
  53.9 0.0 collective-permute-done.2.s_a
  53.9 0.0 collective-permute-done.3.s_b
  53.9 1.8 %shard_map.81.prior = bf16[16,256,128]{2,1,0:T(8,128)(2,1)S(1)} custom-call(f32[8]{0:T(128)S(1)} %copy-done.2, f32[16,3,24,128]{3,2,1,0:T(8,128)S(1)} %get-tuple-element.18.whole, bf16[3,80,128]{2,1,0:T(8,128)(2,1)S(1)} %collective-permute-done.2.s_a, bf16[3,80,128]{2,1,0:T(8,128)(2,1)S(1)} %collective-permute-done.3.s_b, ...), custom_call_target="tpu_custom_call" | custom-call | tf_op jit(solution)/shard_map/pallas_call | solution.py:284
  55.7 6.7 %shard_map.82 = (f32[64,16,512]{2,1,0:T(8,128)S(1)}, bf16[64,16,512]{2,1,0:T(8,128)(2,1)S(1)}, bf16[256,16,128]{2,1,0:T(8,128)(2,1)}) custom-call(bf16[16,256,128]{2,1,0:T(8,128)(2,1)S(1)} %shard_map.81.prior, bf16[16,4096,128]{2,1,0:T(8,128)(2,1)S(1)} %get-tuple-element.24.ops), custom_call_target="tpu_custom_call" | custom-call | tf_op jit(solution)/shard_map/pallas_call | solution.py:313
  62.4 6.3 %collective-permute-start.6 = (bf16[64,16,512]{2,1,0:T(8,128)(2,1)S(1)}, bf16[64,16,512]{2,1,0:T(8,128)(2,1)S(1)}, u32[]{:S(2)}, u32[]{:S(2)}) collective-permute-start(bf16[64,16,512]{2,1,0:T(8,128)(2,1)S(1)} %get-tuple-element.26), channel_id=1, source_target_pairs={{0,1},{1,0},{2,3},{3,2},{4,5},{5,4},{6,7},{7,6},{8,9},{9,8},{10,11... | collective-permute-start | bytes 3145736 | tf_op jit(solution)/shard_map/ppermute | solution.py:340
  68.7 2.3 %collective-permute-done.6 = bf16[64,16,512]{2,1,0:T(8,128)(2,1)S(1)} collective-permute-done((bf16[64,16,512]{2,1,0:T(8,128)(2,1)S(1)}, bf16[64,16,512]{2,1,0:T(8,128)(2,1)S(1)}, u32[]{:S(2)}, u32[]{:S(2)}) %collective-permute-start.6) | collective-permute-done | bytes 1048608 | tf_op jit(solution)/shard_map/ppermute | solution.py:340
  71.0 0.4 add_convert_fusion
  71.4 29.9 %all_to_all.10.pieces = bf16[64,16,512]{2,1,0:T(8,128)(2,1)S(1)} all-to-all(bf16[64,16,512]{2,1,0:T(8,128)(2,1)S(1)} %add_convert_fusion), channel_id=1, replica_groups=mesh['z_lo'=2,'x'=4,'y'=4,'z_hi'=2,'core'=2] {'z_lo','x','y','z_hi'}, dimensions={0} | all-to-all | bytes 2097152 | tf_op jit(solution)/shard_map/all_to_all | solution.py:342
  101.3 0.9 shard_map.83
Async XLA Ops:
  0.6 0.8 copy-start
  1.4 0.7 copy-start.1
  3.5 23.9 %all-to-all-start = ((bf16[128,16,128]{2,1,0:T(8,128)(2,1)}), bf16[128,16,128]{2,1,0:T(8,128)(2,1)S(1)}, u32[]{:S(2)}, u32[]{:S(2)}) async-start(bf16[128,16,128]{2,1,0:T(8,128)(2,1)} %shard_map.77), calls=%async_computation | async-start | bytes 1048576 | tf_op jit(solution)/shard_map/all_to_all | solution.py:365
  27.4 20.7 %copy-start.2 = (f32[8]{0:T(128)S(1)}, f32[8]{0:T(128)}, u32[]{:S(2)}) copy-start(f32[8]{0:T(128)} %table.3) | copy-start | bytes 100
  40.9 7.3 %collective-permute-start.4 = (bf16[3,272,128]{2,1,0:T(8,128)(2,1)S(1)}, bf16[3,272,128]{2,1,0:T(8,128)(2,1)S(1)}, u32[]{:S(2)}, u32[]{:S(2)}) collective-permute-start(bf16[3,272,128]{2,1,0:T(8,128)(2,1)S(1)} %get-tuple-element.22), channel_id=1, source_target_pairs={{0,16},{16,0},{32,48},{48,32},{64,80},{80,64},{96,112},{112,96},{1... | collective-permute-start | bytes 626696 | tf_op jit(solution)/shard_map/ppermute | solution.py:356
  41.0 7.2 %collective-permute-start.5 = (bf16[3,272,128]{2,1,0:T(8,128)(2,1)S(1)}, bf16[3,272,128]{2,1,0:T(8,128)(2,1)S(1)}, u32[]{:S(2)}, u32[]{:S(2)}) collective-permute-start(bf16[3,272,128]{2,1,0:T(8,128)(2,1)S(1)} %get-tuple-element.23), channel_id=1, source_target_pairs={{16,32},{48,64},{80,96},{32,16},{64,48},{96,80},{17,33},{49,65},{8... | collective-permute-start | bytes 626696 | tf_op jit(solution)/shard_map/ppermute | solution.py:355
  41.7 1.3 %collective-permute-start = (bf16[16,16,128]{2,1,0:T(8,128)(2,1)S(1)}, bf16[16,16,128]{2,1,0:T(8,128)(2,1)S(1)}, u32[]{:S(2)}, u32[]{:S(2)}) collective-permute-start(bf16[16,16,128]{2,1,0:T(8,128)(2,1)S(1)} %get-tuple-element.16), channel_id=1, source_target_pairs={{0,1},{1,0},{2,3},{3,2},{4,5},{5,4},{6,7},{7,6},{8,9},{9,8},{10,11... | collective-permute-start | bytes 196616 | tf_op jit(solution)/shard_map/ppermute | solution.py:356
  41.9 1.1 %collective-permute-start.1 = (bf16[16,16,128]{2,1,0:T(8,128)(2,1)S(1)}, bf16[16,16,128]{2,1,0:T(8,128)(2,1)S(1)}, u32[]{:S(2)}, u32[]{:S(2)}) collective-permute-start(bf16[16,16,128]{2,1,0:T(8,128)(2,1)S(1)} %get-tuple-element.17), channel_id=1, source_target_pairs={{1,2},{3,4},{5,6},{7,8},{9,10},{11,12},{13,14},{2,1},{4,3},{6,5},{... | collective-permute-start | bytes 196616 | tf_op jit(solution)/shard_map/ppermute | solution.py:355
  43.1 10.8 %collective-permute-start.2 = (bf16[3,80,128]{2,1,0:T(8,128)(2,1)S(1)}, bf16[3,80,128]{2,1,0:T(8,128)(2,1)S(1)}, u32[]{:S(2)}, u32[]{:S(2)}) collective-permute-start(bf16[3,80,128]{2,1,0:T(8,128)(2,1)S(1)} %get-tuple-element.19), channel_id=1, source_target_pairs={{0,16},{16,0},{32,48},{48,32},{64,80},{80,64},{96,112},{112,96},{1... | collective-permute-start | bytes 184328 | tf_op jit(solution)/shard_map/ppermute | solution.py:356
  47.3 6.6 %collective-permute-start.3 = (bf16[3,80,128]{2,1,0:T(8,128)(2,1)S(1)}, bf16[3,80,128]{2,1,0:T(8,128)(2,1)S(1)}, u32[]{:S(2)}, u32[]{:S(2)}) collective-permute-start(bf16[3,80,128]{2,1,0:T(8,128)(2,1)S(1)} %get-tuple-element.20), channel_id=1, source_target_pairs={{16,32},{48,64},{80,96},{32,16},{64,48},{96,80},{17,33},{49,65},{8... | collective-permute-start | bytes 184328 | tf_op jit(solution)/shard_map/ppermute | solution.py:355
  62.4 8.6 %collective-permute-start.6 = (bf16[64,16,512]{2,1,0:T(8,128)(2,1)S(1)}, bf16[64,16,512]{2,1,0:T(8,128)(2,1)S(1)}, u32[]{:S(2)}, u32[]{:S(2)}) collective-permute-start(bf16[64,16,512]{2,1,0:T(8,128)(2,1)S(1)} %get-tuple-element.26), channel_id=1, source_target_pairs={{0,1},{1,0},{2,3},{3,2},{4,5},{5,4},{6,7},{7,6},{8,9},{9,8},{10,11... | collective-permute-start | bytes 3145736 | tf_op jit(solution)/shard_map/ppermute | solution.py:340

commit v6 on v5

--- a/solution.py
+++ b/solution.py
@@ -84,15 +84,13 @@
     for f in range(FREQ):
         probes[:, f * 128 : f * 128 + 128] = block * masks[f]
     pltpu.make_async_copy(buf.at[slot], buf.at[slot], sems.at[slot]).wait()
-    for f in range(0, FREQ, 2):
-        laid = jnp.swapaxes(buf[slot, f : f + 2].reshape(per * 4, PX, PY), 0, 1)
-        start = pl.multiple_of(group * KW + f * per * 2, per * 4)
-        ops[:, pl.ds(start, per * 4), :] = laid
-        for x in range(0, PX, 2):
-            pair = jnp.concatenate([laid[x], laid[x + 1]], axis=1)
-            both = jnp.dot(probes[:, f * 128 : f * 128 + 256], pair, preferred_element_type=F32)
-            field[x] += both[:, :PY]
-            field[x + 1] += both[:, PY:]
+    laid = jnp.swapaxes(buf[slot].reshape(KW, PX, PY), 0, 1)
+    ops[:, pl.ds(pl.multiple_of(group * KW, KW), KW), :] = laid
+    for x in range(0, PX, 2):
+        pair = jnp.concatenate([laid[x], laid[x + 1]], axis=1)
+        both = jnp.dot(probes[...], pair, preferred_element_type=F32)
+        field[x] += both[:, :PY]
+        field[x + 1] += both[:, PY:]
 
     @pl.when(group == pl.num_programs(0) - 1)
     def _():

time: 103 us -> 103 us (level)
  no operation moved by 1% of the time
where the time goes in v6:
time: 103 us; the launch traced here: 102 us
  Pallas kernels  30.1 us (29%)
  blocking collectives  29.9 us (29%)
  starting transfers between devices  23.9 us (23%)
  waiting for transfers between devices  13.4 us (13%)
  local copies, waits for them, and re-layouts  2.24 us (2%)
  other arithmetic  1.97 us (2%)
    all_to_all x1, blocking collectives, reduced(): pieces = lax.all_to_all(chip, CHIPS, 0, 0, tiled=True)  29.9 us
    pallas_call x1, Pallas kernels, adjoint(): pl.pallas_call(adjoint_body, grid=(NW,), in_specs=[SCALARS, WHOLE, WHOLE,...  13.5 us
    all_to_all x1, starting transfers between devices, on_device(): lax.all_to_all(sent, BOTH, 0, 0, tiled=True).reshape(NW, COLS, per * 2)  11.2 us
    all_to_all x1, waiting for transfers between devices, on_device(): lax.all_to_all(sent, BOTH, 0, 0, tiled=True).reshape(NW, COLS, per * 2)  10.4 us
    pallas_call x1, Pallas kernels, forward(): pl.pallas_call(forward_body, grid=(NW,), in_specs=[WHOLE, WHOLE], out_spe...  6.68 us
    ppermute x1, starting transfers between devices, reduced(): got = lax.ppermute(send, 'core', [(0, 1), (1, 0)])  6.3 us
    pallas_call x1, Pallas kernels, inner_sweeps(): pl.pallas_call(inner_body, in_specs=[SCALARS] + [WHOLE] * 4, out_specs=WH...  5.71 us
    ppermute x3, starting transfers between devices, swapped(): near = lax.ppermute(first, axis, [(i, i ^ 1) for i in range(size)])  4.4 us
  transfers between devices with their start and end apart: 8, of which 4 were waited for; matrix products, arithmetic and copies ran while one was open for 2% of the time, Pallas kernels for 6%

profile of v6, /device:TPU:0, one launch (start us, length us, event | category | flops | bytes accessed | tf_op | source)
XLA Modules:
  0.0 102.2 jit_solution(18135331262841086755)
XLA Ops:
  0.6 0.0 copy-start
  0.6 0.7 copy-done
  1.4 0.0 copy-start.1
  1.4 0.7 copy-done.1
  2.1 1.4 %shard_map.77 = bf16[128,16,128]{2,1,0:T(8,128)(2,1)} custom-call(s32[256]{0:T(256)S(1)} %copy-done.1, bf16[4,2,16,64]{3,2,1,0:T(8,128)(2,1)S(1)} %bitcast.5), custom_call_target="tpu_custom_call" | custom-call | tf_op jit(solution)/shard_map/pallas_call | solution.py:44
  3.5 11.2 %all-to-all-start = ((bf16[128,16,128]{2,1,0:T(8,128)(2,1)}), bf16[128,16,128]{2,1,0:T(8,128)(2,1)S(1)}, u32[]{:S(2)}, u32[]{:S(2)}) async-start(bf16[128,16,128]{2,1,0:T(8,128)(2,1)} %shard_map.77), calls=%async_computation | async-start | bytes 1048576 | tf_op jit(solution)/shard_map/all_to_all | solution.py:363
  14.7 0.8 copy.9.freq
  15.5 0.9 select_reduce_fusion.inv
  16.4 0.7 add_convert_fusion.1.classes
  17.1 10.4 %all-to-all-done = bf16[128,16,128]{2,1,0:T(8,128)(2,1)S(1)} async-done(((bf16[128,16,128]{2,1,0:T(8,128)(2,1)}), bf16[128,16,128]{2,1,0:T(8,128)(2,1)S(1)}, u32[]{:S(2)}, u32[]{:S(2)}) %all-to-all-start) | async-done | bytes 524320 | tf_op jit(solution)/shard_map/all_to_all | solution.py:363
  27.4 0.0 copy-start.2
  27.4 13.5 %shard_map.78 = (bf16[16,4096,128]{2,1,0:T(8,128)(2,1)S(1)}, f32[16,256,128]{2,1,0:T(8,128)S(1)}, f32[16,3,24,128]{3,2,1,0:T(8,128)S(1)}, bf16[16,16,128]{2,1,0:...) custom-call(s32[512]{0:T(512)S(1)} %select_reduce_fusion.inv, ...), custom_call_target="tpu_custom_call" | custom-call | tf_op jit(solution)/shard_map/pallas_call | solution.py:130
  41.0 0.1 collective-permute-start.4
  41.1 0.7 collective-permute-start.5
  41.7 0.2 collective-permute-start
  41.9 0.7 collective-permute-start.1
  42.6 0.5 collective-permute-done.y_a
  43.1 0.0 collective-permute-done.1.y_b
  43.1 0.1 shard_map.79
  43.2 4.1 %collective-permute-start.2 = (bf16[3,80,128]{2,1,0:T(8,128)(2,1)S(1)}, bf16[3,80,128]{2,1,0:T(8,128)(2,1)S(1)}, u32[]{:S(2)}, u32[]{:S(2)}) collective-permute-start(bf16[3,80,128]{2,1,0:T(8,128)(2,1)S(1)} %get-tuple-element.19), channel_id=1, source_target_pairs={{0,16},{16,0},{32,48},{48,32},{64,80},{80,64},{96,112},{112,96},{1... | collective-permute-start | bytes 184328 | tf_op jit(solution)/shard_map/ppermute | solution.py:354
  47.3 0.7 collective-permute-start.3
  48.0 0.2 collective-permute-done.4.x_a
  48.2 0.0 collective-permute-done.5.x_b
  48.2 0.0 copy-done.2
  48.2 5.7 %shard_map.80.inner = bf16[16,256,128]{2,1,0:T(8,128)(2,1)S(1)} custom-call(f32[8]{0:T(128)S(1)} %copy-done.2, f32[16,256,128]{2,1,0:T(8,128)S(1)} %get-tuple-element.21.field, bf16[3,272,128]{2,1,0:T(8,128)(2,1)S(1)} %collective-permute-done.4.x_a, bf16[3,272,128]{2,1,0:T(8,128)(2,1)S(1)} %collective-permute-done.5.x_b, f32[16,128]{1,0:T(8,128)S(1)} %add_convert_fusion.1.classes), custom_call_target="tpu_custom_call" | custom-call | tf_op jit(solution)/shard_map/pallas_call | solution.py:249
  53.9 0.0 collective-permute-done.2.s_a
  54.0 0.0 collective-permute-done.3.s_b
  54.0 1.8 %shard_map.81.prior = bf16[16,256,128]{2,1,0:T(8,128)(2,1)S(1)} custom-call(f32[8]{0:T(128)S(1)} %copy-done.2, f32[16,3,24,128]{3,2,1,0:T(8,128)S(1)} %get-tuple-element.18.whole, bf16[3,80,128]{2,1,0:T(8,128)(2,1)S(1)} %collective-permute-done.2.s_a, bf16[3,80,128]{2,1,0:T(8,128)(2,1)S(1)} %collective-permute-done.3.s_b, ...), custom_call_target="tpu_custom_call" | custom-call | tf_op jit(solution)/shard_map/pallas_call | solution.py:282
  55.8 6.7 %shard_map.82 = (f32[64,16,512]{2,1,0:T(8,128)S(1)}, bf16[64,16,512]{2,1,0:T(8,128)(2,1)S(1)}, bf16[256,16,128]{2,1,0:T(8,128)(2,1)}) custom-call(bf16[16,256,128]{2,1,0:T(8,128)(2,1)S(1)} %shard_map.81.prior, bf16[16,4096,128]{2,1,0:T(8,128)(2,1)S(1)} %get-tuple-element.24.ops), custom_call_target="tpu_custom_call" | custom-call | tf_op jit(solution)/shard_map/pallas_call | solution.py:311
  62.5 6.3 %collective-permute-start.6 = (bf16[64,16,512]{2,1,0:T(8,128)(2,1)S(1)}, bf16[64,16,512]{2,1,0:T(8,128)(2,1)S(1)}, u32[]{:S(2)}, u32[]{:S(2)}) collective-permute-start(bf16[64,16,512]{2,1,0:T(8,128)(2,1)S(1)} %get-tuple-element.26), channel_id=1, source_target_pairs={{0,1},{1,0},{2,3},{3,2},{4,5},{5,4},{6,7},{7,6},{8,9},{9,8},{10,11... | collective-permute-start | bytes 3145736 | tf_op jit(solution)/shard_map/ppermute | solution.py:338
  68.8 2.3 %collective-permute-done.6 = bf16[64,16,512]{2,1,0:T(8,128)(2,1)S(1)} collective-permute-done((bf16[64,16,512]{2,1,0:T(8,128)(2,1)S(1)}, bf16[64,16,512]{2,1,0:T(8,128)(2,1)S(1)}, u32[]{:S(2)}, u32[]{:S(2)}) %collective-permute-start.6) | collective-permute-done | bytes 1048608 | tf_op jit(solution)/shard_map/ppermute | solution.py:338
  71.1 0.4 add_convert_fusion
  71.5 29.9 %all_to_all.10.pieces = bf16[64,16,512]{2,1,0:T(8,128)(2,1)S(1)} all-to-all(bf16[64,16,512]{2,1,0:T(8,128)(2,1)S(1)} %add_convert_fusion), channel_id=1, replica_groups=mesh['z_lo'=2,'x'=4,'y'=4,'z_hi'=2,'core'=2] {'z_lo','x','y','z_hi'}, dimensions={0} | all-to-all | bytes 2097152 | tf_op jit(solution)/shard_map/all_to_all | solution.py:340
  101.4 0.9 shard_map.83
Async XLA Ops:
  0.6 0.8 copy-start
  1.4 0.7 copy-start.1
  3.5 23.9 %all-to-all-start = ((bf16[128,16,128]{2,1,0:T(8,128)(2,1)}), bf16[128,16,128]{2,1,0:T(8,128)(2,1)S(1)}, u32[]{:S(2)}, u32[]{:S(2)}) async-start(bf16[128,16,128]{2,1,0:T(8,128)(2,1)} %shard_map.77), calls=%async_computation | async-start | bytes 1048576 | tf_op jit(solution)/shard_map/all_to_all | solution.py:363
  27.4 20.8 %copy-start.2 = (f32[8]{0:T(128)S(1)}, f32[8]{0:T(128)}, u32[]{:S(2)}) copy-start(f32[8]{0:T(128)} %table.3) | copy-start | bytes 100
  41.0 7.3 %collective-permute-start.4 = (bf16[3,272,128]{2,1,0:T(8,128)(2,1)S(1)}, bf16[3,272,128]{2,1,0:T(8,128)(2,1)S(1)}, u32[]{:S(2)}, u32[]{:S(2)}) collective-permute-start(bf16[3,272,128]{2,1,0:T(8,128)(2,1)S(1)} %get-tuple-element.22), channel_id=1, source_target_pairs={{0,16},{16,0},{32,48},{48,32},{64,80},{80,64},{96,112},{112,96},{1... | collective-permute-start | bytes 626696 | tf_op jit(solution)/shard_map/ppermute | solution.py:354
  41.1 7.2 %collective-permute-start.5 = (bf16[3,272,128]{2,1,0:T(8,128)(2,1)S(1)}, bf16[3,272,128]{2,1,0:T(8,128)(2,1)S(1)}, u32[]{:S(2)}, u32[]{:S(2)}) collective-permute-start(bf16[3,272,128]{2,1,0:T(8,128)(2,1)S(1)} %get-tuple-element.23), channel_id=1, source_target_pairs={{16,32},{48,64},{80,96},{32,16},{64,48},{96,80},{17,33},{49,65},{8... | collective-permute-start | bytes 626696 | tf_op jit(solution)/shard_map/ppermute | solution.py:353
  41.7 1.3 %collective-permute-start = (bf16[16,16,128]{2,1,0:T(8,128)(2,1)S(1)}, bf16[16,16,128]{2,1,0:T(8,128)(2,1)S(1)}, u32[]{:S(2)}, u32[]{:S(2)}) collective-permute-start(bf16[16,16,128]{2,1,0:T(8,128)(2,1)S(1)} %get-tuple-element.16), channel_id=1, source_target_pairs={{0,1},{1,0},{2,3},{3,2},{4,5},{5,4},{6,7},{7,6},{8,9},{9,8},{10,11... | collective-permute-start | bytes 196616 | tf_op jit(solution)/shard_map/ppermute | solution.py:354
  41.9 1.2 %collective-permute-start.1 = (bf16[16,16,128]{2,1,0:T(8,128)(2,1)S(1)}, bf16[16,16,128]{2,1,0:T(8,128)(2,1)S(1)}, u32[]{:S(2)}, u32[]{:S(2)}) collective-permute-start(bf16[16,16,128]{2,1,0:T(8,128)(2,1)S(1)} %get-tuple-element.17), channel_id=1, source_target_pairs={{1,2},{3,4},{5,6},{7,8},{9,10},{11,12},{13,14},{2,1},{4,3},{6,5},{... | collective-permute-start | bytes 196616 | tf_op jit(solution)/shard_map/ppermute | solution.py:353
  43.2 10.8 %collective-permute-start.2 = (bf16[3,80,128]{2,1,0:T(8,128)(2,1)S(1)}, bf16[3,80,128]{2,1,0:T(8,128)(2,1)S(1)}, u32[]{:S(2)}, u32[]{:S(2)}) collective-permute-start(bf16[3,80,128]{2,1,0:T(8,128)(2,1)S(1)} %get-tuple-element.19), channel_id=1, source_target_pairs={{0,16},{16,0},{32,48},{48,32},{64,80},{80,64},{96,112},{112,96},{1... | collective-permute-start | bytes 184328 | tf_op jit(solution)/shard_map/ppermute | solution.py:354
  47.3 6.6 %collective-permute-start.3 = (bf16[3,80,128]{2,1,0:T(8,128)(2,1)S(1)}, bf16[3,80,128]{2,1,0:T(8,128)(2,1)S(1)}, u32[]{:S(2)}, u32[]{:S(2)}) collective-permute-start(bf16[3,80,128]{2,1,0:T(8,128)(2,1)S(1)} %get-tuple-element.20), channel_id=1, source_target_pairs={{16,32},{48,64},{80,96},{32,16},{64,48},{96,80},{17,33},{49,65},{8... | collective-permute-start | bytes 184328 | tf_op jit(solution)/shard_map/ppermute | solution.py:353
  62.5 8.6 %collective-permute-start.6 = (bf16[64,16,512]{2,1,0:T(8,128)(2,1)S(1)}, bf16[64,16,512]{2,1,0:T(8,128)(2,1)S(1)}, u32[]{:S(2)}, u32[]{:S(2)}) collective-permute-start(bf16[64,16,512]{2,1,0:T(8,128)(2,1)S(1)} %get-tuple-element.26), channel_id=1, source_target_pairs={{0,1},{1,0},{2,3},{3,2},{4,5},{5,4},{6,7},{7,6},{8,9},{9,8},{10,11... | collective-permute-start | bytes 3145736 | tf_op jit(solution)/shard_map/ppermute | solution.py:338
